TPU v7x, 32 devices: a whole 2x2x4 slice. The times are simulated.
32 devices in a mesh: dp: 16 (over z, y, x), tensor: 2 (over core).
Axes of the slice: x: 2, y: 2, z: 4, core: 2. Of those that a mesh axis runs over, the one named last changes fastest.
Arguments:
- activations: bfloat16 [24576, 768], P('dp'), may hold values from -6 to 6
- cotangent: bfloat16 [24576, 768], P('dp'), may hold values from -6 to 6
- token_weight: int32 [24576], P('dp'), may hold values from 1 to 4
- lengths: int32 [48], P('dp'), may hold values from 64 to 512, as said below
- step_count: int32 [1], replicated, may hold values from 1 to 20
- inward_weight: float32 [3, 768, 768], P(None, 'dp', 'tensor'), may hold values from -0.21875 to 0.21875
- output_weight: float32 [768, 768], P('tensor', 'dp'), may hold values from -2 to 2
- up_weight: float32 [768, 3072], P('dp', 'tensor'), may hold values from -0.21875 to 0.21875
- down_weight: float32 [3072, 768], P('tensor', 'dp'), may hold values from -0.109375 to 0.109375
- heads_bias: float32 [2, 48, 16], P(None, 'tensor', 'dp'), may hold values from -3 to 3
- hidden_bias: float32 [192, 16], P('tensor', 'dp'), may hold values from -3 to 3
- norm_vectors: float32 [6, 768], P(None, 'dp'), may hold values from -0.9 to 1.6
- inward_first: float32 [3, 768, 768], P(None, 'dp', 'tensor'), may hold values from -1792 to 1792
- output_first: float32 [768, 768], P('tensor', 'dp'), may hold values from -192 to 192
- up_first: float32 [768, 3072], P('dp', 'tensor'), may hold values from -512 to 512
- down_first: float32 [3072, 768], P('tensor', 'dp'), may hold values from -1024 to 1024
- heads_first: float32 [2, 48, 16], P(None, 'tensor', 'dp'), may hold values from -1792 to 1792
- hidden_first: float32 [192, 16], P('tensor', 'dp'), may hold values from -512 to 512
- norm_first: float32 [6, 768], P(None, 'dp'), may hold values from -1280 to 1280
- inward_second: float32 [3, 768, 768], P(None, 'dp', 'tensor'), may hold values from 98304 to 393216
- output_second: float32 [768, 768], P('tensor', 'dp'), may hold values from 1152 to 4608
- up_second: float32 [768, 3072], P('dp', 'tensor'), may hold values from 8847.36 to 35389.44
- down_second: float32 [3072, 768], P('tensor', 'dp'), may hold values from 29491.2 to 117964.8
- heads_second: float32 [2, 48, 16], P(None, 'tensor', 'dp'), may hold values from 98304 to 393216
- hidden_second: float32 [192, 16], P('tensor', 'dp'), may hold values from 8847.36 to 35389.44
- norm_second: float32 [6, 768], P(None, 'dp'), may hold values from 55296 to 221184
Outputs:
- layer_output: bfloat16 [24576, 768], P('dp')
- input_grad: float32 [24576, 768], P('dp')
- new_inward: float32 [3, 768, 768], P(None, 'dp', 'tensor')
- new_inward_first: float32 [3, 768, 768], P(None, 'dp', 'tensor')
- new_inward_second: float32 [3, 768, 768], P(None, 'dp', 'tensor')
- new_output: float32 [768, 768], P('tensor', 'dp')
- new_output_first: float32 [768, 768], P('tensor', 'dp')
- new_output_second: float32 [768, 768], P('tensor', 'dp')
- new_up: float32 [768, 3072], P('dp', 'tensor')
- new_up_first: float32 [768, 3072], P('dp', 'tensor')
- new_up_second: float32 [768, 3072], P('dp', 'tensor')
- new_down: float32 [3072, 768], P('tensor', 'dp')
- new_down_first: float32 [3072, 768], P('tensor', 'dp')
- new_down_second: float32 [3072, 768], P('tensor', 'dp')
- new_heads: float32 [2, 48, 16], P(None, 'tensor', 'dp')
- new_heads_first: float32 [2, 48, 16], P(None, 'tensor', 'dp')
- new_heads_second: float32 [2, 48, 16], P(None, 'tensor', 'dp')
- new_hidden: float32 [192, 16], P('tensor', 'dp')
- new_hidden_first: float32 [192, 16], P('tensor', 'dp')
- new_hidden_second: float32 [192, 16], P('tensor', 'dp')
- new_norm: float32 [6, 768], P(None, 'dp')
- new_norm_first: float32 [6, 768], P(None, 'dp')
- new_norm_second: float32 [6, 768], P(None, 'dp')
Inputs may be any that keep to these rules, and one draw needn't show every extreme that they name: Sequence s holds lengths[s] real tokens followed by padding; some sequence is full and some has an eighth of 512.
All inputs are finite; a program needn't handle non-finite values.
Results may differ from a plain program's by a relative error of at most 0.018.
Values may be sent and summed in bfloat16 or wider, within the bound.
No kernel may reach another device: no remote copies, remote signals or barrier semaphores. Data moves between devices by JAX's collectives and lax.ppermute only.
A program may use at most 192 MiB of HBM per device.

v0:
```python
from functools import partial
import math

import jax
import jax.numpy as jnp
from jax import lax
from jax.sharding import PartitionSpec as P

D = 768
HEAD_DIM = 64
FF = 3072
LEN = 512


norm_epsilon = 1e-12


def normalize(total_in):
    average = jnp.mean(total_in, axis=-1, keepdims=True)
    centred = total_in - average
    inverse = lax.rsqrt(jnp.mean(centred * centred, axis=-1, keepdims=True) + norm_epsilon)
    return (centred * inverse, inverse)


def norm_back(incoming, normed, inverse, gain):
    scaled = incoming * gain
    return inverse * (
        scaled
        - jnp.mean(scaled, axis=-1, keepdims=True)
        - normed * jnp.mean(scaled * normed, axis=-1, keepdims=True)
    )


def gelu_slope(hidden):
    return 0.5 * (
        1.0 + lax.erf(hidden * 0.7071067811865476)
    ) + hidden * 0.3989422804014327 * jnp.exp(-0.5 * hidden * hidden)


def masked_scores(queries, key_rows, length, score_scale):
    scores = (
        jnp.einsum("qhd,khd->hqk", queries, key_rows, preferred_element_type=jnp.float32)
        * score_scale
    )
    live_mask = lax.broadcasted_iota(jnp.int32, (1, 1, key_rows.shape[0]), 2) < length
    return jnp.where(live_mask, scores, -jnp.inf)


def probabilities(scores):
    row_max = jnp.max(scores, axis=-1, keepdims=True)
    weights = jnp.exp(scores - row_max)
    weight_sum = jnp.sum(weights, axis=-1, keepdims=True)
    return (weights / weight_sum, row_max + jnp.log(weight_sum))


def attend(item_parts, score_scale):
    queries, key_rows, values, length = item_parts
    weights, log_total = probabilities(masked_scores(queries, key_rows, length, score_scale))
    context = jnp.einsum(
        "hqk,khd->qhd", weights.astype(jnp.bfloat16), values, preferred_element_type=jnp.float32
    )
    return (context.astype(jnp.bfloat16), log_total)


def attend_back(item_parts, score_scale, rebuild):
    queries, key_rows, values, length, log_total, context_grad = item_parts
    scores = masked_scores(queries, key_rows, length, score_scale)
    weights, unused_total = probabilities(scores)
    low_weights = weights.astype(jnp.bfloat16)
    value_grads = jnp.einsum(
        "hqk,qhd->khd", low_weights, context_grad, preferred_element_type=jnp.float32
    ).astype(jnp.bfloat16)
    weight_grads = jnp.einsum(
        "qhd,khd->hqk", context_grad, values, preferred_element_type=jnp.float32
    )
    score_grads = (
        weights * (weight_grads - jnp.sum(weights * weight_grads, axis=-1, keepdims=True))
    ).astype(jnp.bfloat16)
    query_grads = (
        jnp.einsum("hqk,khd->qhd", score_grads, key_rows, preferred_element_type=jnp.float32)
        * score_scale
    ).astype(jnp.bfloat16)
    key_grads = (
        jnp.einsum("hqk,qhd->khd", score_grads, queries, preferred_element_type=jnp.float32)
        * score_scale
    ).astype(jnp.bfloat16)
    context = jnp.einsum(
        "hqk,khd->qhd", low_weights, values, preferred_element_type=jnp.float32
    ).astype(jnp.bfloat16)
    return (query_grads, key_grads, value_grads, context)


def adamw(
    master,
    gradient,
    first_moment,
    second_moment,
    step_rate,
    decay_rate,
    first_correct,
    second_correct,
):
    first_new = 0.5 * first_moment + 0.5 * gradient
    second_new = 0.5 * second_moment + 0.5 * gradient * gradient
    moved = first_new / first_correct / (jnp.sqrt(second_new / second_correct) + 1e-08)
    return (master - step_rate * (moved + decay_rate * master), first_new, second_new)


def per_device(
    activations,
    cotangent,
    token_weight,
    lengths,
    step_count,
    inward_weight,
    output_weight,
    up_weight,
    down_weight,
    heads_bias,
    hidden_bias,
    norm_vectors,
    inward_first,
    output_first,
    up_first,
    down_first,
    heads_first,
    hidden_first,
    norm_first,
    inward_second,
    output_second,
    up_second,
    down_second,
    heads_second,
    hidden_second,
    norm_second,
):
    data_size = lax.axis_size("dp")
    gathered = (
        lax.all_gather(inward_weight.astype(jnp.bfloat16), "dp", axis=1, tiled=True),
        lax.all_gather(output_weight.astype(jnp.bfloat16), "dp", axis=1, tiled=True),
        lax.all_gather(up_weight.astype(jnp.bfloat16), "dp", axis=0, tiled=True),
        lax.all_gather(down_weight.astype(jnp.bfloat16), "dp", axis=1, tiled=True),
        lax.all_gather(heads_bias.astype(jnp.bfloat16), "dp", axis=2, tiled=True),
        lax.all_gather(hidden_bias.astype(jnp.bfloat16), "dp", axis=1, tiled=True),
        lax.all_gather(norm_vectors.astype(jnp.bfloat16), "dp", axis=1, tiled=True),
    )
    inward, outward, upward, downward, head_low, hidden_low, vector_low = gathered
    local_width = inward.shape[2]
    local_heads = local_width // HEAD_DIM
    head_biases = head_low.astype(jnp.float32).reshape(2, local_width)
    hidden_biases = hidden_low.astype(jnp.float32).reshape(-1)
    vectors = vector_low.astype(jnp.float32)
    row_count = activations.shape[0]
    seq_count = row_count // LEN
    score_scale = 1.0 / math.sqrt(HEAD_DIM)
    head_shape = (seq_count, LEN, local_heads, HEAD_DIM)

    def project(source):
        mixed = jnp.einsum("td,kde->kte", source, inward, preferred_element_type=jnp.float32)
        queries = (mixed[0] + head_biases[0]).astype(jnp.bfloat16).reshape(head_shape)
        key_rows = mixed[1].astype(jnp.bfloat16).reshape(head_shape)
        values = (mixed[2] + head_biases[1]).astype(jnp.bfloat16).reshape(head_shape)
        return (queries, key_rows, values)

    def expand(source):
        hidden = jnp.dot(source, upward, preferred_element_type=jnp.float32) + hidden_biases
        return (hidden, jax.nn.gelu(hidden, approximate=False).astype(jnp.bfloat16))

    queries, key_rows, values = project(activations)
    context_heads, log_total = lax.map(
        partial(attend, score_scale=score_scale), (queries, key_rows, values, lengths)
    )
    context = context_heads.reshape(row_count, local_width)
    branch_part = jnp.dot(context, outward, preferred_element_type=jnp.float32)
    branch = lax.psum(branch_part.astype(jnp.bfloat16), "tensor").astype(jnp.float32)
    first_sum = branch + vectors[0] + activations.astype(jnp.float32)
    normed_first, inverse_first = normalize(first_sum)
    middle = normed_first * vectors[1] + vectors[2]
    middle_low = middle.astype(jnp.bfloat16)
    hidden, active = expand(middle_low)
    down_part = jnp.dot(active, downward, preferred_element_type=jnp.float32)
    down_sum = lax.psum(down_part.astype(jnp.bfloat16), "tensor").astype(jnp.float32)
    second_sum = down_sum + vectors[3] + middle
    normed_second, inverse_second = normalize(second_sum)
    output_rows = (normed_second * vectors[4] + vectors[5]).astype(jnp.bfloat16)
    live_mask = (lax.broadcasted_iota(jnp.int32, (seq_count, LEN), 1) < lengths[:, None]).reshape(
        row_count
    )
    output_grad = (
        cotangent.astype(jnp.float32)
        * (token_weight * live_mask.astype(jnp.int32)).astype(jnp.float32)[:, None]
    )
    grad_gain_two = jnp.sum(output_grad * normed_second, axis=0)
    grad_bias_two = jnp.sum(output_grad, axis=0)
    second_grad = norm_back(output_grad, normed_second, inverse_second, vectors[4])
    grad_down_bias = jnp.sum(second_grad, axis=0)
    second_low = second_grad.astype(jnp.bfloat16)
    hidden, active = expand(lax.optimization_barrier(middle_low))
    downward_grad = jnp.einsum("tf,td->fd", active, second_low, preferred_element_type=jnp.float32)
    active_grad = jnp.einsum("td,fd->tf", second_low, downward, preferred_element_type=jnp.float32)
    hidden_grad = (active_grad * gelu_slope(hidden)).astype(jnp.bfloat16)
    hidden_bias_grad = jnp.sum(hidden_grad.astype(jnp.float32), axis=0)
    upward_grad = jnp.einsum(
        "td,tf->df", middle_low, hidden_grad, preferred_element_type=jnp.float32
    )
    middle_part = jnp.einsum("tf,df->td", hidden_grad, upward, preferred_element_type=jnp.float32)
    middle_grad = (
        lax.psum(middle_part.astype(jnp.bfloat16), "tensor").astype(jnp.float32) + second_grad
    )
    grad_gain_one = jnp.sum(middle_grad * normed_first, axis=0)
    grad_bias_one = jnp.sum(middle_grad, axis=0)
    first_grad = norm_back(middle_grad, normed_first, inverse_first, vectors[1])
    grad_out_bias = jnp.sum(first_grad, axis=0)
    first_low = first_grad.astype(jnp.bfloat16)
    context_grad = (
        jnp.einsum("td,ed->te", first_low, outward, preferred_element_type=jnp.float32)
        .astype(jnp.bfloat16)
        .reshape(head_shape)
    )
    queries, key_rows, values = project(lax.optimization_barrier(activations))
    query_grads, key_grads, value_grads, context_heads = lax.map(
        partial(attend_back, score_scale=score_scale, rebuild=True),
        (queries, key_rows, values, lengths, log_total, context_grad),
    )
    context = context_heads.reshape(row_count, local_width)
    outward_grad = jnp.einsum("te,td->ed", context, first_low, preferred_element_type=jnp.float32)
    stacked_grads = jnp.stack(
        [
            query_grads.reshape(row_count, local_width),
            key_grads.reshape(row_count, local_width),
            value_grads.reshape(row_count, local_width),
        ]
    )
    heads_grad = jnp.stack(
        [
            jnp.sum(stacked_grads[0].astype(jnp.float32), axis=0),
            jnp.sum(stacked_grads[2].astype(jnp.float32), axis=0),
        ]
    )
    inward_grad = jnp.einsum(
        "td,kte->kde", activations, stacked_grads, preferred_element_type=jnp.float32
    )
    input_part = jnp.einsum(
        "kte,kde->td", stacked_grads, inward, preferred_element_type=jnp.float32
    )
    norm_stack = jnp.stack(
        [grad_out_bias, grad_gain_one, grad_bias_one, grad_down_bias, grad_gain_two, grad_bias_two]
    )
    norm_outgoing = jnp.zeros_like(norm_stack)
    summed_input, summed_norm = (
        lax.psum(input_part.astype(jnp.bfloat16), "tensor").astype(jnp.float32),
        lax.psum(norm_outgoing.astype(jnp.bfloat16), "tensor").astype(jnp.float32),
    )
    input_grad = summed_input + first_grad
    heads_shaped = heads_grad.reshape(2, local_width // data_size, data_size)
    reduced = (
        lax.psum_scatter(inward_grad, "dp", scatter_dimension=1, tiled=True),
        lax.psum_scatter(outward_grad, "dp", scatter_dimension=1, tiled=True),
        lax.psum_scatter(upward_grad, "dp", scatter_dimension=0, tiled=True),
        lax.psum_scatter(downward_grad, "dp", scatter_dimension=1, tiled=True),
        lax.psum_scatter(heads_shaped, "dp", scatter_dimension=2, tiled=True),
        lax.psum_scatter(
            hidden_bias_grad.reshape(-1, data_size), "dp", scatter_dimension=1, tiled=True
        ),
        lax.psum_scatter(norm_stack, "dp", scatter_dimension=1, tiled=True),
    )
    step_value = step_count[0].astype(jnp.float32)
    first_correct = 1.0 - jnp.power(0.5, step_value)
    second_correct = 1.0 - jnp.power(0.5, step_value)
    plan = (step_value + 4.0) / 12.0
    rates = (D ** (-0.5), (6 * D // LEN) ** (-0.5), D ** (-0.5), FF ** (-0.5), 0.5, 0.5, 0.3)
    decays = (0.01, 0.01, 0.01, 0.01, 0.0, 0.0, 0.0)
    masters = (
        inward_weight,
        output_weight,
        up_weight,
        down_weight,
        heads_bias,
        hidden_bias,
        norm_vectors,
    )
    firsts = (
        inward_first,
        output_first,
        up_first,
        down_first,
        heads_first,
        hidden_first,
        norm_first,
    )
    seconds = (
        inward_second,
        output_second,
        up_second,
        down_second,
        heads_second,
        hidden_second,
        norm_second,
    )
    results = [output_rows, input_grad]
    for index_of in range(7):
        updated = adamw(
            masters[index_of],
            reduced[index_of],
            firsts[index_of],
            seconds[index_of],
            rates[index_of] * plan,
            decays[index_of],
            first_correct,
            second_correct,
        )
        results.extend(updated)
    return (
        results[0],
        results[1],
        results[2],
        results[3],
        results[4],
        results[5],
        results[6],
        results[7],
        results[8],
        results[9],
        results[10],
        results[11],
        results[12],
        results[13],
        results[14],
        results[15],
        results[16],
        results[17],
        results[18],
        results[19],
        results[20],
        results[21],
        results[22],
    )


def solution(mesh):
    in_specs = (
        P("dp", None),
        P("dp", None),
        P("dp"),
        P("dp"),
        P(),
        P(None, "dp", "tensor"),
        P("tensor", "dp"),
        P("dp", "tensor"),
        P("tensor", "dp"),
        P(None, "tensor", "dp"),
        P("tensor", "dp"),
        P(None, "dp"),
        P(None, "dp", "tensor"),
        P("tensor", "dp"),
        P("dp", "tensor"),
        P("tensor", "dp"),
        P(None, "tensor", "dp"),
        P("tensor", "dp"),
        P(None, "dp"),
        P(None, "dp", "tensor"),
        P("tensor", "dp"),
        P("dp", "tensor"),
        P("tensor", "dp"),
        P(None, "tensor", "dp"),
        P("tensor", "dp"),
        P(None, "dp"),
    )
    out_specs = (
        P("dp", None),
        P("dp", None),
        P(None, "dp", "tensor"),
        P(None, "dp", "tensor"),
        P(None, "dp", "tensor"),
        P("tensor", "dp"),
        P("tensor", "dp"),
        P("tensor", "dp"),
        P("dp", "tensor"),
        P("dp", "tensor"),
        P("dp", "tensor"),
        P("tensor", "dp"),
        P("tensor", "dp"),
        P("tensor", "dp"),
        P(None, "tensor", "dp"),
        P(None, "tensor", "dp"),
        P(None, "tensor", "dp"),
        P("tensor", "dp"),
        P("tensor", "dp"),
        P("tensor", "dp"),
        P(None, "dp"),
        P(None, "dp"),
        P(None, "dp"),
    )
    return jax.shard_map(
        per_device, mesh=mesh, in_specs=in_specs, out_specs=out_specs, check_vma=False
    )
```

profile of v0, /device:TPU:0, one launch (start us, length us, event | category | flops | bytes accessed | tf_op | source)
XLA Modules:
  0.0 1210.8 jit_solution(600087267559365601)
XLA Ops:
  9.6 42.4 %all_gather.22 = bf16[2,24,16]{1,0,2:T(2,128)(2,1)S(1)} all-gather(bf16[2,24,1]{1,0,2:T(2,128)(2,1)S(1)} %convert_element_type.167), channel_id=1, replica_groups=mesh['dp'=16,'tensor'=2] {'dp'}, dimensions={2}, use_global_device_ids=true | all-gather | bytes 1632 | tf_op jit(solution)/shard_map/all_gather | solution.py:143
  53.2 42.4 %all_gather.23 = bf16[384,768]{0,1:T(8,128)(2,1)} all-gather(bf16[384,48]{0,1:T(8,128)(2,1)S(1)} %convert_element_type.172), channel_id=1, replica_groups=mesh['dp'=16,'tensor'=2] {'dp'}, dimensions={1}, use_global_device_ids=true | all-gather | bytes 626688 | tf_op jit(solution)/shard_map/all_gather | solution.py:140
  95.6 5.2 convolution_bitcast_fusion.1
  113.2 4.9 squeeze.47
  118.1 4.8 squeeze.46
  127.7 4.8 squeeze.45
  132.6 4.4 add_convert_fusion.2
  138.2 4.8 squeeze.44
  143.1 4.4 add_convert_fusion.1
  148.9 34.4 %while.26 = (s32[]{:T(128)}, bf16[3,512,6,64]{1,3,2,0:T(8,128)(2,1)S(1)}, bf16[3,512,6,64]{1,3,2,0:T(8,128)(2,1)}, s32[3]{0:T(128)S(1)}, bf16[3,512,6,64]{1,3,2,...) while((s32[]{:T(128)}, bf16[3,512,6,64]{1,3,2,0:T(8,128)(2,1)S(1)}, ...), condition=%wide.region_3.4_spmd, body=%wide.region_0.3_spmd.sunk | while | flops 412288000 | bytes 14187621 | solution.py:170
  150.1 6.7 fusion.303
  161.6 6.7 fusion.303
  173.0 6.7 fusion.303
  189.2 36.9 %all-gather.1 = bf16[16,1,96]{2,1,0:T(2,128)(2,1)S(1)} all-gather(bf16[1,1,96]{2,1,0:T(2,128)(2,1)S(1)} %convert_bitcast_fusion.1), channel_id=1, replica_groups=mesh['dp'=16,'tensor'=2] {'dp'}, dimensions={0}, use_global_device_ids=true | all-gather | bytes 3264 | tf_op jit(solution)/shard_map/all_gather | solution.py:144
  226.2 36.4 %all-gather = bf16[16,48,6]{1,2,0:T(8,128)(2,1)S(1)} all-gather(bf16[1,48,6]{1,2,0:T(8,128)(2,1)S(1)} %convert_bitcast_fusion), channel_id=1, replica_groups=mesh['dp'=16,'tensor'=2] {'dp'}, dimensions={0}, use_global_device_ids=true | all-gather | bytes 9792 | tf_op jit(solution)/shard_map/all_gather | solution.py:145
  269.5 4.0 all-gather.8.cloned.1.call-done
  273.6 63.8 %all-gather.10.cloned.1.call-done = bf16[1536,768]{0,1:T(8,128)(2,1)} async-done(((bf16[1536,48]{0,1:T(8,128)(2,1)}), bf16[1536,768]{0,1:T(8,128)(2,1)}) %all-gather.10.cloned.1.call-update) | async-done | bytes 2359312 | tf_op jit(solution)/shard_map/all_gather | solution.py:142
  337.4 30.4 %convolution_convert_fusion.1 = bf16[1536,768]{1,0:T(8,128)(2,1)} fusion(bf16[1536,768]{0,1:T(8,128)(2,1)} %all-gather.10.cloned.1.call-done, bf16[1536,768]{1,0:T(8,128)(2,1)} %fusion.146, bf16[768,1536]{1,0:T(8,128)(2,1)} %all-gather.8.cloned.1.call-done, f32[1536]{0:T(1024)S(1)} %reshape.189), kind=kOutput, calls=%fused_computation.165 | convolution fusion | flops 7404650496 | bytes 9443328 | tf_op jit(solution)/shard_map/dot_general | solution.py:181
  368.0 9.9 convolution_add_fusion
  377.8 10.2 all-reduce.12.cloned.1.call-done
  388.1 4.1 fusion.236
  400.4 7.5 convert_reduce_fusion
  410.0 5.1 convolution_convert_fusion
  426.2 11.9 all-reduce.14.cloned.1.call-done
  438.2 6.9 multiply_reduce_fusion.2
  445.1 6.8 fusion.229
  460.1 4.5 copy.201
  467.1 66.1 %while.27 = (s32[]{:T(128)}, bf16[3,512,6,64]{1,3,2,0:T(8,128)(2,1)S(1)}, bf16[3,512,6,64]{1,3,2,0:T(8,128)(2,1)}, bf16[3,512,6,64]{1,3,2,0:T(8,128)(2,1)S(1)}, ...) while((s32[]{:T(128)}, ...), condition=%wide.region_19.20_spmd, body=%wide.region_15.19_spmd.sunk | while | flops 1232730112 | bytes 88181952 | solution.py:221
  469.5 6.0 fusion.315
  475.5 4.5 fusion.319
  491.6 6.0 fusion.315
  497.6 4.5 fusion.319
  513.6 6.0 fusion.315
  519.6 4.5 fusion.319
  542.8 4.2 reshape.204
  550.6 5.1 reshape.202
  559.2 5.1 reshape.203
  568.1 4.5 bitcast_convert_fusion
  572.6 6.8 fusion.152
  579.4 6.4 copy.210
  585.9 7.8 fusion.258
  593.8 30.1 %fusion.144 = f32[1536,768]{0,1:T(8,128)} fusion(f32[1536,1536]{1,0:T(8,128)} %convolution_add_fusion, f32[1536,768]{1,0:T(8,128)} %copy-done.6), kind=kOutput, calls=%fused_computation.156 | convolution fusion | flops 3778412544 | bytes 18874368 | tf_op jit(solution)/shard_map/tf,td->fd/dot_general | solution.py:199
  626.9 77.4 %all-reduce.3 = (f32[2,24,16]{1,0,2:T(2,128)S(1)}, f32[96,16]{1,0:T(8,128)S(1)}) all-reduce(f32[2,24,16]{1,0,2:T(2,128)S(1)} %copy.215, f32[96,16]{1,0:T(8,128)S(1)} %reshape.188), channel_id=6, replica_groups=mesh['dp'=16,'tensor'=2] {'dp'}, use_global_device_ids=true, to_apply=%region_27.28.clone | all-reduce | flops 2304 | bytes 18432
  710.0 20.2 %all-reduce.16.cloned.1.call-done = bf16[1536,768]{1,0:T(8,128)(2,1)} async-done(((bf16[1536,768]{1,0:T(8,128)(2,1)}), bf16[1536,768]{1,0:T(8,128)(2,1)}) %all-reduce.16.cloned.1.call-update) | async-done | bytes 2359312 | tf_op jit(solution)/shard_map/psum | solution.py:251
  730.2 5.7 convert_add_fusion
  735.9 180.0 %all-reduce.18.cloned.1.call-done = f32[3,768,384]{2,0,1:T(4,128)} async-done(((f32[3,768,384]{2,0,1:T(4,128)}), f32[3,768,384]{2,0,1:T(4,128)}) %all-reduce.18.cloned.1.call-update) | async-done | bytes 3538960
  917.9 141.1 %reduce-scatter.10.cloned.1.call-done = f32[48,1536]{1,0:T(8,128)} async-done(((f32[768,1536]{1,0:T(8,128)}), f32[48,1536]{1,0:T(8,128)}) %reduce-scatter.10.cloned.1.call-update) | async-done | bytes 294928 | tf_op jit(solution)/shard_map/reduce_scatter | solution.py:259
  1061.0 140.8 %reduce-scatter.12.cloned.1.call-done = f32[1536,48]{0,1:T(8,128)} async-done(((f32[1536,768]{0,1:T(8,128)}), f32[1536,48]{0,1:T(8,128)}) %reduce-scatter.12.cloned.1.call-update) | async-done | bytes 294928 | tf_op jit(solution)/shard_map/reduce_scatter | solution.py:260
  (290 shorter events, 150.6 us)
Async XLA Ops:
  7.2 88.4 %all-gather.6.cloned.1.call-start = ((), (), s32[]{:S(2)}) async-start(), calls=%async_computation.4 | async-start | bytes 1880064 | tf_op jit(solution)/shard_map/all_gather | solution.py:139
  8.9 254.1 %all-reduce.10.cloned.1.call-start = ((), (), s32[]{:S(2)}) async-start(), calls=%async_computation.5 | async-start | bytes 4718592 | tf_op jit(solution)/shard_map/psum | solution.py:175
  184.7 41.4 %copy-start.41 = (f32[6,48]{1,0:T(8,128)S(1)}, f32[6,48]{1,0:T(8,128)}, u32[]{:S(2)}) copy-start(f32[6,48]{1,0:T(8,128)} %param.41) | copy-start | bytes 3460
  187.6 86.0 %all-gather.8.cloned.1.call-start = ((), (), s32[]{:S(2)}) async-start(), calls=%async_computation.6 | async-start | bytes 2506752 | tf_op jit(solution)/shard_map/all_gather | solution.py:141
  188.4 149.0 %all-gather.10.cloned.1.call-start = ((), (), s32[]{:S(2)}) async-start(), calls=%async_computation.7 | async-start | bytes 2506752 | tf_op jit(solution)/shard_map/all_gather | solution.py:142
  189.1 199.0 %all-reduce.12.cloned.1.call-start = ((), (), s32[]{:S(2)}) async-start(), calls=%async_computation.8 | async-start | bytes 4718592 | tf_op jit(solution)/shard_map/psum | solution.py:182
  262.9 125.2 %copy-start.33 = (f32[768]{0:T(1024)}, f32[768]{0:T(1024)S(1)}, u32[]{:S(2)}) copy-start(f32[768]{0:T(1024)S(1)} %get-tuple-element.285) | copy-start | bytes 9220
  262.9 125.2 %copy-start.35 = (f32[768]{0:T(1024)}, f32[768]{0:T(1024)S(1)}, u32[]{:S(2)}) copy-start(f32[768]{0:T(1024)S(1)} %get-tuple-element.284) | copy-start | bytes 9220
  269.5 98.3 %copy-start.51 = (s32[3]{0:T(128)S(1)}, s32[3]{0:T(128)}, u32[]{:S(2)}) copy-start(s32[3]{0:T(128)} %param.33) | copy-start | bytes 40
  269.5 98.4 %copy-start.44 = (s32[1536]{0:T(1024)S(1)}, s32[1536]{0:T(1024)}, u32[]{:S(2)}) copy-start(s32[1536]{0:T(1024)} %param.32) | copy-start | bytes 18436
  367.8 70.4 %all-reduce.14.cloned.1.call-start = ((), (), s32[]{:S(2)}) async-start(), calls=%async_computation.9 | async-start | bytes 4718592 | tf_op jit(solution)/shard_map/psum | solution.py:208
  400.3 7.5 copy-start.6
  400.3 9.6 copy-start.56
  415.1 291.8 %reduce-scatter.14.cloned.1.call-start = ((), (), s32[]{:S(2)}) async-start(), calls=%async_computation.14 | async-start | bytes 417792
  419.1 7.2 copy-start.40
  419.1 7.2 copy-start.39
  419.1 19.1 %copy-start.34 = (f32[768]{0:T(1024)S(1)}, f32[768]{0:T(1024)}, u32[]{:S(2)}) copy-start(f32[768]{0:T(1024)} %copy-done.33) | copy-start | bytes 9220
  419.1 19.1 %copy-start.36 = (f32[768]{0:T(1024)S(1)}, f32[768]{0:T(1024)}, u32[]{:S(2)}) copy-start(f32[768]{0:T(1024)} %copy-done.35) | copy-start | bytes 9220
  438.2 6.9 copy-start.10
  445.1 7.9 copy-start.17
  453.0 255.3 %reduce-scatter.8.cloned.1.call-start = ((), (), s32[]{:S(2)}) async-start(), calls=%async_computation.11 | async-start | bytes 1253376 | tf_op jit(solution)/shard_map/reduce_scatter | solution.py:258
  460.1 7.0 copy-start.11
  533.2 13.8 %copy-start.7 = (bf16[3,512,6,64]{1,3,2,0:T(8,128)(2,1)}, bf16[3,512,6,64]{1,3,2,0:T(8,128)(2,1)S(1)}, u32[]{:S(2)}) copy-start(bf16[3,512,6,64]{1,3,2,0:T(8,128)(2,1)S(1)} %get-tuple-element.111) | copy-start | bytes 3538948
  538.9 191.3 %all-reduce.16.cloned.1.call-start = ((), (), s32[]{:S(2)}) async-start(), calls=%async_computation.10 | async-start | bytes 4718592 | tf_op jit(solution)/shard_map/psum | solution.py:251
  572.6 343.3 %all-reduce.18.cloned.1.call-start = ((), (), s32[]{:S(2)}) async-start(), calls=%async_computation.15 | async-start | bytes 9437184
  585.8 473.1 %reduce-scatter.10.cloned.1.call-start = ((), (), s32[]{:S(2)}) async-start(), calls=%async_computation.12 | async-start | bytes 5013504 | tf_op jit(solution)/shard_map/reduce_scatter | solution.py:259
  593.8 608.0 %reduce-scatter.12.cloned.1.call-start = ((), (), s32[]{:S(2)}) async-start(), calls=%async_computation.13 | async-start | bytes 5013504 | tf_op jit(solution)/shard_map/reduce_scatter | solution.py:260
  623.9 81.2 %copy-start.53 = (f32[96,1]{0,1:T(1,128)S(1)}, f32[96,1]{0,1:T(1,128)}, u32[]{:S(2)}) copy-start(f32[96,1]{0,1:T(1,128)} %param.40) | copy-start | bytes 1156
  623.9 81.2 %copy-start.54 = (f32[96,1]{0,1:T(1,128)S(1)}, f32[96,1]{0,1:T(1,128)}, u32[]{:S(2)}) copy-start(f32[96,1]{0,1:T(1,128)} %param.54) | copy-start | bytes 1156
  623.9 81.2 %copy-start.55 = (f32[96,1]{0,1:T(1,128)S(1)}, f32[96,1]{0,1:T(1,128)}, u32[]{:S(2)}) copy-start(f32[96,1]{0,1:T(1,128)} %param.47) | copy-start | bytes 1156
  623.9 81.7 %copy-start.47 = (f32[2,24,1]{1,2,0:T(1,128)S(1)}, f32[2,24,1]{1,2,0:T(1,128)}, u32[]{:S(2)}) copy-start(f32[2,24,1]{1,2,0:T(1,128)} %param.39) | copy-start | bytes 580
  623.9 81.7 %copy-start.48 = (f32[2,24,1]{1,2,0:T(1,128)S(1)}, f32[2,24,1]{1,2,0:T(1,128)}, u32[]{:S(2)}) copy-start(f32[2,24,1]{1,2,0:T(1,128)} %param.53) | copy-start | bytes 580
  623.9 81.7 %copy-start.49 = (f32[2,24,1]{1,2,0:T(1,128)S(1)}, f32[2,24,1]{1,2,0:T(1,128)}, u32[]{:S(2)}) copy-start(f32[2,24,1]{1,2,0:T(1,128)} %param.46) | copy-start | bytes 580
  623.9 83.7 %copy-start.42 = (f32[6,48]{1,0:T(8,128)S(1)}, f32[6,48]{1,0:T(8,128)}, u32[]{:S(2)}) copy-start(f32[6,48]{1,0:T(8,128)} %param.41) | copy-start | bytes 3460
  624.0 83.7 %copy-start.45 = (f32[6,48]{1,0:T(8,128)S(1)}, f32[6,48]{1,0:T(8,128)}, u32[]{:S(2)}) copy-start(f32[6,48]{1,0:T(8,128)} %param.55) | copy-start | bytes 3460
  624.0 83.7 %copy-start.46 = (f32[6,48]{1,0:T(8,128)S(1)}, f32[6,48]{1,0:T(8,128)}, u32[]{:S(2)}) copy-start(f32[6,48]{1,0:T(8,128)} %param.48) | copy-start | bytes 3460
  624.0 84.4 %copy-start.30 = (f32[384,48]{0,1:T(8,128)S(1)}, f32[384,48]{0,1:T(8,128)}, u32[]{:S(2)}) copy-start(f32[384,48]{0,1:T(8,128)} %param.36) | copy-start | bytes 221188
  624.0 84.3 %copy-start.37 = (f32[384,48]{0,1:T(8,128)S(1)}, f32[384,48]{0,1:T(8,128)}, u32[]{:S(2)}) copy-start(f32[384,48]{0,1:T(8,128)} %param.50) | copy-start | bytes 221188
  624.0 84.3 %copy-start.38 = (f32[384,48]{0,1:T(8,128)S(1)}, f32[384,48]{0,1:T(8,128)}, u32[]{:S(2)}) copy-start(f32[384,48]{0,1:T(8,128)} %param.43) | copy-start | bytes 221188
  709.9 207.0 %copy-start.24 = (f32[3,48,384]{2,1,0:T(8,128)S(1)}, f32[3,48,384]{2,1,0:T(8,128)}, u32[]{:S(2)}) copy-start(f32[3,48,384]{2,1,0:T(8,128)} %param.35) | copy-start | bytes 663556
  709.9 207.0 %copy-start.31 = (f32[3,48,384]{2,1,0:T(8,128)S(1)}, f32[3,48,384]{2,1,0:T(8,128)}, u32[]{:S(2)}) copy-start(f32[3,48,384]{2,1,0:T(8,128)} %param.49) | copy-start | bytes 663556
  709.9 207.0 %copy-start.32 = (f32[3,48,384]{2,1,0:T(8,128)S(1)}, f32[3,48,384]{2,1,0:T(8,128)}, u32[]{:S(2)}) copy-start(f32[3,48,384]{2,1,0:T(8,128)} %param.42) | copy-start | bytes 663556
  709.9 349.0 %copy-start.20 = (f32[48,1536]{1,0:T(8,128)S(1)}, f32[48,1536]{1,0:T(8,128)}, u32[]{:S(2)}) copy-start(f32[48,1536]{1,0:T(8,128)} %param.37) | copy-start | bytes 884740
  709.9 349.0 %copy-start.26 = (f32[48,1536]{1,0:T(8,128)S(1)}, f32[48,1536]{1,0:T(8,128)}, u32[]{:S(2)}) copy-start(f32[48,1536]{1,0:T(8,128)} %param.51) | copy-start | bytes 884740
  710.0 349.0 %copy-start.27 = (f32[48,1536]{1,0:T(8,128)S(1)}, f32[48,1536]{1,0:T(8,128)}, u32[]{:S(2)}) copy-start(f32[48,1536]{1,0:T(8,128)} %param.44) | copy-start | bytes 884740
  710.0 491.8 %copy-start.22 = (f32[1536,48]{0,1:T(8,128)S(1)}, f32[1536,48]{0,1:T(8,128)}, u32[]{:S(2)}) copy-start(f32[1536,48]{0,1:T(8,128)} %param.38) | copy-start | bytes 884740
  710.0 491.8 %copy-start.28 = (f32[1536,48]{0,1:T(8,128)S(1)}, f32[1536,48]{0,1:T(8,128)}, u32[]{:S(2)}) copy-start(f32[1536,48]{0,1:T(8,128)} %param.52) | copy-start | bytes 884740
  710.0 491.7 %copy-start.29 = (f32[1536,48]{0,1:T(8,128)S(1)}, f32[1536,48]{0,1:T(8,128)}, u32[]{:S(2)}) copy-start(f32[1536,48]{0,1:T(8,128)} %param.45) | copy-start | bytes 884740
  (33 other events, 132.5 us)
Sparse Core Ops, SparseCore 0:
  11.3 64.4 all-gather.5
  187.7 18.9 all-reduce.9
  210.1 63.4 all-gather.7
  276.8 60.5 all-gather.9
  367.9 20.1 all-reduce.11
  415.2 22.9 all-reduce.13
  453.1 124.3 reduce-scatter.13
  582.2 124.7 reduce-scatter.7
  709.4 20.7 all-reduce.15
  735.8 180.1 all-reduce.17
  921.1 137.8 reduce-scatter.9
  1064.0 137.7 reduce-scatter.11
where the time goes:
time: 1220 us; the launch traced here: 1210 us
  waiting for transfers between devices  572 us (47%)
  blocking collectives  235 us (19%)
  matrix products  201 us (16%)
  local copies, waits for them, and re-layouts  114 us (9%)
  other arithmetic  70.8 us (6%)
  between operations  16.7 us (1%)
    unnamed x14, waiting for transfers between devices  180 us
    reduce_scatter x1, waiting for transfers between devices, per_device(): lax.psum_scatter(upward_grad, 'dp', scatter_dimension=0, tiled=True)  141 us
    reduce_scatter x1, waiting for transfers between devices, per_device(): lax.psum_scatter(downward_grad, 'dp', scatter_dimension=1, tiled=True)  141 us
    unnamed x1, blocking collectives  77.4 us
    all_gather x1, waiting for transfers between devices, per_device(): lax.all_gather(down_weight.astype(jnp.bfloat16), 'dp', axis=1, tiled=True)  63.8 us
    all_gather x1, blocking collectives, per_device(): lax.all_gather(heads_bias.astype(jnp.bfloat16), 'dp', axis=2, tiled=True)  42.4 us
    all_gather x1, blocking collectives, per_device(): lax.all_gather(output_weight.astype(jnp.bfloat16), 'dp', axis=1, tiled=True)  42.4 us
    sub x6, matrix products, probabilities(): weights = jnp.exp(scores - row_max)  38.2 us
  transfers between devices with their start and end apart: 12, of which 8 were waited for; matrix products, arithmetic and copies ran while one was open for 18% of the time, Pallas kernels for 0%

commit v1 on v0

v1 whole, which is shorter than its diff:
```python
from functools import partial
import math

import jax
import jax.numpy as jnp
from jax import lax
from jax.experimental import pallas as pl
from jax.experimental.pallas import tpu as pltpu
from jax.sharding import PartitionSpec as P

D = 768
HEAD_DIM = 64
FF = 3072
LEN = 512
LANES = 128
HIDDEN_BLOCK = 768

norm_epsilon = 1e-12
low = jnp.bfloat16
full = jnp.float32


def dot_nn(left, right):
    return lax.dot_general(left, right, (((1,), (0,)), ((), ())), preferred_element_type=full)


def dot_nt(left, right):
    return lax.dot_general(left, right, (((1,), (1,)), ((), ())), preferred_element_type=full)


def column_sum(values):
    return jnp.sum(values, axis=0, keepdims=True)


def row_mean(values):
    return jnp.mean(values, axis=-1, keepdims=True)


def normalize(total_in):
    centred = total_in - row_mean(total_in)
    inverse = lax.rsqrt(row_mean(centred * centred) + norm_epsilon)
    return (centred * inverse, inverse)


def norm_back(incoming, normed, inverse, gain):
    scaled = incoming * gain
    return inverse * (scaled - row_mean(scaled) - normed * row_mean(scaled * normed))


def cost(flops, moved, exps=0):
    return pl.CostEstimate(flops=int(flops), bytes_accessed=int(moved), transcendentals=int(exps))


def params(**extra):
    return pltpu.CompilerParams(vmem_limit_bytes=58 * 1024 * 1024, **extra)


def shape(dims, kind):
    return jax.ShapeDtypeStruct(dims, kind)


def after(value, *others):
    return lax.optimization_barrier((value,) + others)[0]


def hop(value, offset, size):
    return lax.ppermute(value, "dp", [(d, d ^ offset) for d in range(size)])


def swap_cores(value):
    return lax.ppermute(value, "tensor", [(0, 1), (1, 0)])


def split_columns(width):
    return -(-width // (2 * LANES)) * LANES


def gather_planes(shard, size):
    found = [shard] + [hop(shard, 4 * k, size) for k in range(1, size // 4)]
    return found


def gather_pieces(found, size):
    stacked = jnp.stack(found)
    cut = split_columns(stacked.shape[2])
    own_a, own_b = lax.optimization_barrier((stacked[..., :cut], stacked[..., cut:]))
    y_a, x_b = hop(own_a, 2, size), hop(own_b, 1, size)
    x_a, y_b = hop(own_a, 1, size), hop(own_b, 2, size)
    xy_a, xy_b = hop(y_a, 1, size), hop(x_b, 2, size)
    return ((own_a, x_a, y_a, xy_a), (own_b, x_b, y_b, xy_b))


def place_kernel(me_ref, *refs):
    out_ref = refs[-1]
    rows = refs[0].shape[1]
    cut = refs[0].shape[2]
    for plane in range(4):
        for k in range(refs[0].shape[0]):
            start = pl.multiple_of((me_ref[0] ^ (4 * k + plane)) * rows, 16)
            out_ref[pl.ds(start, rows), :cut] = refs[plane][k]
            out_ref[pl.ds(start, rows), cut:] = refs[4 + plane][k]


def place(pieces, me):
    flat = pieces[0] + pieces[1]
    layers, rows, cut = flat[0].shape
    width = cut + flat[4].shape[2]
    total = 4 * layers * rows
    return pl.pallas_call(
        place_kernel,
        out_shape=shape((total, width), low),
        grid_spec=pltpu.PrefetchScalarGridSpec(
            num_scalar_prefetch=1,
            grid=(1,),
            in_specs=[pl.BlockSpec(piece.shape, lambda i, m: (0, 0, 0)) for piece in flat],
            out_specs=pl.BlockSpec((total, width), lambda i, m: (0, 0)),
        ),
        compiler_params=params(),
        cost_estimate=cost(0, 4 * total * width),
        name="place",
    )(me, *flat)


def reduce_start(pieces, size):
    sent_a, kept_a, sent_b, kept_b = pieces
    return (hop(sent_a, 1, size), kept_a, hop(sent_b, 2, size), kept_b)


def reduce_middle(state, size):
    got_a, kept_a, got_b, kept_b = state
    next_a, next_b = lax.optimization_barrier((kept_a[1] + got_a[1], kept_b[1] + got_b[1]))
    return (kept_a, got_a, hop(next_a, 2, size), kept_b, got_b, hop(next_b, 1, size))


def reduce_last(state, size):
    kept_a, got_a, more_a, kept_b, got_b, more_b = state

    def total(kept, got, more):
        return kept[0].astype(full) + got[0].astype(full) + more.astype(full)

    sum_a, sum_b = total(kept_a, got_a, more_a), total(kept_b, got_b, more_b)
    layers = sum_a.shape[0]
    outgoing = lax.optimization_barrier(
        tuple(
            jnp.concatenate([sum_a[k].astype(low), sum_b[k].astype(low)], axis=-1)
            for k in range(1, layers)
        )
    )
    arrived = [hop(piece, 4 * (k + 1), size) for k, piece in enumerate(outgoing)]
    own = jnp.concatenate([sum_a[0], sum_b[0]], axis=-1)
    return (own, arrived)


def reduce_sum(state):
    own, arrived = state
    for piece in arrived:
        own = own + piece.astype(full)
    return own


def attend_kernel(length_ref, x_ref, w_ref, bias_ref, qkv_ref, weight_ref, context_ref):
    length = length_ref[pl.program_id(1)]
    mixed = dot_nn(x_ref[...], w_ref[...])
    queries = (mixed[:, :LANES] + bias_ref[0:1, :]).astype(low)
    key_rows = mixed[:, LANES : 2 * LANES].astype(low)
    values_full = mixed[:, 2 * LANES :] + bias_ref[1:2, :]
    values = values_full.astype(low)
    qkv_ref[:, :LANES] = queries
    qkv_ref[:, LANES : 2 * LANES] = key_rows
    qkv_ref[:, 2 * LANES :] = values
    values_t = values_full.T.astype(low)
    rows = queries.shape[0]
    lane = lax.broadcasted_iota(jnp.int32, (rows, LANES), 1)
    live = lax.broadcasted_iota(jnp.int32, (rows, 1), 0) < length
    scaled = queries * (1.0 / math.sqrt(HEAD_DIM))
    parts = []
    for head in range(2):
        picked = jnp.where((lane >= HEAD_DIM) == bool(head), scaled, jnp.zeros_like(scaled))
        scores = jnp.where(live, dot_nt(key_rows, picked), -jnp.inf)
        grown = jnp.exp(scores - jnp.max(scores, axis=0, keepdims=True))
        weights = (grown * (1.0 / jnp.sum(grown, axis=0, keepdims=True))).astype(low)
        weight_ref[0, head] = weights
        parts.append(dot_nn(values_t[head * HEAD_DIM : (head + 1) * HEAD_DIM, :], weights))
    context_ref[...] = jnp.concatenate(parts, axis=0).T.astype(low)


def attend(lengths, source, inward, biases):
    count = source.shape[0] // LEN
    groups = biases.shape[1] // LANES
    rows = source.shape[0]
    width = 3 * LANES
    return pl.pallas_call(
        attend_kernel,
        out_shape=(
            shape((rows, groups * width), low),
            shape((groups * count, 2, LEN, LEN), low),
            shape((rows, groups * LANES), low),
        ),
        grid_spec=pltpu.PrefetchScalarGridSpec(
            num_scalar_prefetch=1,
            grid=(groups, count),
            in_specs=[
                pl.BlockSpec((LEN, D), lambda g, s, n: (s, 0)),
                pl.BlockSpec((D, width), lambda g, s, n: (0, g)),
                pl.BlockSpec((2, LANES), lambda g, s, n: (0, g)),
            ],
            out_specs=(
                pl.BlockSpec((LEN, width), lambda g, s, n: (s, g)),
                pl.BlockSpec((1, 2, LEN, LEN), lambda g, s, n: (g * count + s, 0, 0, 0)),
                pl.BlockSpec((LEN, LANES), lambda g, s, n: (s, g)),
            ),
        ),
        compiler_params=params(),
        cost_estimate=cost(
            2 * rows * D * groups * width + 8 * groups * count * LEN * LEN * LANES,
            groups * count * 2 * LEN * LEN * 2,
            groups * count * 2 * LEN * LEN,
        ),
        name="attend",
    )(lengths, source, inward, biases)


def attend_back_kernel(qkv_ref, weight_ref, grad_ref, out_ref, sum_ref):
    @pl.when(pl.program_id(1) == 0)
    def _():
        sum_ref[...] = jnp.zeros_like(sum_ref)

    queries = qkv_ref[:, :LANES]
    key_rows = qkv_ref[:, LANES : 2 * LANES]
    values = qkv_ref[:, 2 * LANES :]
    grads = grad_ref[...]
    keys_t = key_rows.astype(full).T.astype(low)
    rows = queries.shape[0]
    lane = lax.broadcasted_iota(jnp.int32, (rows, LANES), 1)
    score_scale = 1.0 / math.sqrt(HEAD_DIM)
    query_parts, key_parts, value_parts = [], [], []
    for head in range(2):
        picked = jnp.where((lane >= HEAD_DIM) == bool(head), grads, jnp.zeros_like(grads))
        weights = weight_ref[0, head]
        wide = weights.astype(full)
        mixed = wide * dot_nt(values, picked)
        score_grads = (mixed - wide * jnp.sum(mixed, axis=0, keepdims=True)).astype(low)
        value_parts.append(dot_nn(weights, grads))
        key_parts.append(dot_nn(score_grads, queries))
        query_parts.append(
            dot_nn(keys_t[head * HEAD_DIM : (head + 1) * HEAD_DIM, :], score_grads)
        )
    first = lane < HEAD_DIM
    query_grads = (jnp.concatenate(query_parts, axis=0).T * score_scale).astype(low)
    key_grads = (jnp.where(first, key_parts[0], key_parts[1]) * score_scale).astype(low)
    value_grads = jnp.where(first, value_parts[0], value_parts[1]).astype(low)
    out_ref[:, :LANES] = query_grads
    out_ref[:, LANES : 2 * LANES] = key_grads
    out_ref[:, 2 * LANES :] = value_grads
    sum_ref[0:1, :] += column_sum(query_grads.astype(full))
    sum_ref[1:2, :] += column_sum(value_grads.astype(full))


def attend_back(qkv, weights, grads, group):
    rows = qkv.shape[0]
    count = rows // LEN
    width = 3 * LANES
    return pl.pallas_call(
        attend_back_kernel,
        out_shape=(shape((rows, width), low), shape((2, LANES), full)),
        grid=(1, count),
        in_specs=[
            pl.BlockSpec((LEN, width), lambda g, s: (s, group)),
            pl.BlockSpec((1, 2, LEN, LEN), lambda g, s: (group * count + s, 0, 0, 0)),
            pl.BlockSpec((LEN, LANES), lambda g, s: (s, group)),
        ],
        out_specs=(
            pl.BlockSpec((LEN, width), lambda g, s: (s, 0)),
            pl.BlockSpec((2, LANES), lambda g, s: (0, 0)),
        ),
        compiler_params=params(),
        cost_estimate=cost(
            16 * count * LEN * LEN * LANES, count * 2 * LEN * LEN * 2 + 4 * rows * width
        ),
        name="attend_back",
    )(qkv, weights, grads)


def outward_kernel(context_ref, w_ref, out_ref):
    out_ref[...] = dot_nt(context_ref[...], w_ref[...]).astype(low)


def outward_part(context, outward, item):
    width = context.shape[1]
    return pl.pallas_call(
        outward_kernel,
        out_shape=shape((LEN, D), low),
        grid=(1,),
        in_specs=[
            pl.BlockSpec((LEN, width), lambda i: (item, 0)),
            pl.BlockSpec((D, width), lambda i: (0, 0)),
        ],
        out_specs=pl.BlockSpec((LEN, D), lambda i: (0, 0)),
        compiler_params=params(),
        cost_estimate=cost(2 * LEN * D * width, 2 * (LEN * D + LEN * width + D * width)),
        name="outward",
    )(context, outward)


def expand_kernel(
    mine_ref, other_ref, x_ref, vector_ref, bias_ref, up_ref, down_ref,
    active_in, slope_in, middle_in, normed_in, inverse_in,
    part_ref, active_ref, slope_ref, middle_ref, normed_ref, inverse_ref, total_ref, held_ref,
):
    step = pl.program_id(0)

    @pl.when(step == 0)
    def _():
        summed = (
            mine_ref[...].astype(full)
            + other_ref[...].astype(full)
            + vector_ref[0:1, :]
            + x_ref[...].astype(full)
        )
        normed, inverse = normalize(summed)
        normed_ref[...] = normed
        inverse_ref[...] = inverse
        held = (normed * vector_ref[1:2, :] + vector_ref[2:3, :]).astype(low)
        held_ref[...] = held
        middle_ref[...] = held

    hidden = dot_nn(held_ref[...], up_ref[...]) + bias_ref[...]
    half = 0.5 + 0.5 * lax.erf(hidden * 0.7071067811865476)
    active = (hidden * half).astype(low)
    active_ref[...] = active
    slope_ref[...] = (
        half + hidden * 0.3989422804014327 * jnp.exp(-0.5 * hidden * hidden)
    ).astype(low)
    part = dot_nt(active, down_ref[...])

    @pl.when(step == 0)
    def _():
        total_ref[...] = part

    @pl.when(step > 0)
    def _():
        total_ref[...] += part

    @pl.when(step == pl.num_programs(0) - 1)
    def _():
        part_ref[...] = total_ref[...].astype(low)


any_spec = pl.BlockSpec(memory_space=pl.ANY)


def expand(mine, other, source, vectors, hidden_bias, upward, downward, held, item):
    rows, hidden = source.shape[0], upward.shape[1]
    block = HIDDEN_BLOCK
    fixed = pl.BlockSpec((LEN, D), lambda j: (0, 0))
    row = pl.BlockSpec((LEN, D), lambda j: (item, 0))
    wide = pl.BlockSpec((LEN, block), lambda j: (item, j))
    weight = pl.BlockSpec((D, block), lambda j: (0, j))
    outs = (
        shape((LEN, D), low),
        shape((rows, hidden), low),
        shape((rows, hidden), low),
        shape((rows, D), low),
        shape((rows, D), full),
        shape((rows, 1), full),
    )
    first = held is None
    kernel = expand_kernel
    if first:
        kernel = lambda *refs: expand_kernel(*refs[:7], *([None] * 5), *refs[7:])
    return pl.pallas_call(
        kernel,
        out_shape=outs,
        grid=(hidden // block,),
        in_specs=[
            fixed,
            fixed,
            row,
            pl.BlockSpec(vectors.shape, lambda j: (0, 0)),
            pl.BlockSpec((1, block), lambda j: (0, j)),
            weight,
            weight,
        ]
        + ([] if first else [any_spec] * 5),
        out_specs=(fixed, wide, wide, row, row, pl.BlockSpec((LEN, 1), lambda j: (item, 0))),
        scratch_shapes=[pltpu.VMEM((LEN, D), full), pltpu.VMEM((LEN, D), low)],
        input_output_aliases={} if first else {7 + i: 1 + i for i in range(5)},
        compiler_params=params(),
        cost_estimate=cost(
            4 * LEN * D * hidden, 4 * D * hidden + 4 * LEN * hidden, 2 * LEN * hidden
        ),
        name="expand",
    )(mine, other, source, vectors, hidden_bias, upward, downward, *(() if first else held))


def contract_kernel(
    mine_ref, other_ref, normed_ref, cotangent_ref, scale_ref, vector_ref, slope_ref,
    up_ref, down_ref, out_in, wide_in, low_in, hidden_in,
    part_ref, sum_ref, hidden_sum_ref, out_ref, wide_ref, low_ref, hidden_ref,
    total_ref, held_ref,
):
    step = pl.program_id(0)

    @pl.when(step == 0)
    def _():
        middle = normed_ref[...] * vector_ref[1:2, :] + vector_ref[2:3, :]
        summed = (
            mine_ref[...].astype(full) + other_ref[...].astype(full) + vector_ref[3:4, :] + middle
        )
        normed, inverse = normalize(summed)
        out_ref[...] = (normed * vector_ref[4:5, :] + vector_ref[5:6, :]).astype(low)
        incoming = cotangent_ref[...].astype(full) * scale_ref[...]
        second = norm_back(incoming, normed, inverse, vector_ref[4:5, :])
        sum_ref[0:1, :] = column_sum(second)
        sum_ref[1:2, :] = column_sum(incoming * normed)
        sum_ref[2:3, :] = column_sum(incoming)
        wide_ref[...] = second
        held = second.astype(low)
        held_ref[...] = held
        low_ref[...] = held

    hidden_grad = (dot_nn(held_ref[...], down_ref[...]) * slope_ref[...].astype(full)).astype(low)
    hidden_ref[...] = hidden_grad
    hidden_sum_ref[...] = column_sum(hidden_grad.astype(full))
    part = dot_nt(hidden_grad, up_ref[...])

    @pl.when(step == 0)
    def _():
        total_ref[...] = part

    @pl.when(step > 0)
    def _():
        total_ref[...] += part

    @pl.when(step == pl.num_programs(0) - 1)
    def _():
        part_ref[...] = total_ref[...].astype(low)


def contract(mine, other, normed, cotangent, scale, vectors, slope, upward, downward, held, item):
    rows, hidden = slope.shape
    block = HIDDEN_BLOCK
    fixed = pl.BlockSpec((LEN, D), lambda j: (0, 0))
    row = pl.BlockSpec((LEN, D), lambda j: (item, 0))
    wide = pl.BlockSpec((LEN, block), lambda j: (item, j))
    weight = pl.BlockSpec((D, block), lambda j: (0, j))
    outs = (
        shape((LEN, D), low),
        shape((3, D), full),
        shape((1, hidden), full),
        shape((rows, D), low),
        shape((rows, D), full),
        shape((rows, D), low),
        shape((rows, hidden), low),
    )
    first = held is None
    kernel = contract_kernel
    if first:
        kernel = lambda *refs: contract_kernel(*refs[:9], *([None] * 4), *refs[9:])
    return pl.pallas_call(
        kernel,
        out_shape=outs,
        grid=(hidden // block,),
        in_specs=[
            fixed,
            fixed,
            row,
            row,
            pl.BlockSpec((LEN, 1), lambda j: (item, 0)),
            pl.BlockSpec(vectors.shape, lambda j: (0, 0)),
            wide,
            weight,
            weight,
        ]
        + ([] if first else [any_spec] * 4),
        out_specs=(
            fixed,
            pl.BlockSpec((3, D), lambda j: (0, 0)),
            pl.BlockSpec((1, block), lambda j: (0, j)),
            row,
            row,
            row,
            wide,
        ),
        scratch_shapes=[pltpu.VMEM((LEN, D), full), pltpu.VMEM((LEN, D), low)],
        input_output_aliases={} if first else {9 + i: 3 + i for i in range(4)},
        compiler_params=params(),
        cost_estimate=cost(4 * LEN * D * hidden, 4 * D * hidden + 4 * LEN * hidden),
        name="contract",
    )(
        mine, other, normed, cotangent, scale, vectors, slope, upward, downward,
        *(() if first else held),
    )


def first_back_kernel(
    mine_ref, other_ref, second_ref, normed_ref, inverse_ref, vector_ref, w_ref,
    wide_in, low_in, grad_in, sum_ref, wide_ref, low_ref, grad_ref,
):
    incoming = mine_ref[...].astype(full) + other_ref[...].astype(full) + second_ref[...]
    normed = normed_ref[...]
    first = norm_back(incoming, normed, inverse_ref[...], vector_ref[1:2, :])
    sum_ref[0:1, :] = column_sum(first)
    sum_ref[1:2, :] = column_sum(incoming * normed)
    sum_ref[2:3, :] = column_sum(incoming)
    wide_ref[...] = first
    held = first.astype(low)
    low_ref[...] = held
    grad_ref[...] = dot_nn(held, w_ref[...]).astype(low)


def first_back(mine, other, second, normed, inverse, vectors, outward, held, item):
    rows, width = second.shape[0], outward.shape[1]
    fixed = pl.BlockSpec((LEN, D), lambda j: (0, 0))
    row = pl.BlockSpec((LEN, D), lambda j: (item, 0))
    first = held is None
    kernel = first_back_kernel
    if first:
        kernel = lambda *refs: first_back_kernel(*refs[:7], *([None] * 3), *refs[7:])
    return pl.pallas_call(
        kernel,
        out_shape=(
            shape((3, D), full),
            shape((rows, D), full),
            shape((rows, D), low),
            shape((rows, width), low),
        ),
        grid=(1,),
        in_specs=[
            fixed,
            fixed,
            row,
            row,
            pl.BlockSpec((LEN, 1), lambda j: (item, 0)),
            pl.BlockSpec(vectors.shape, lambda j: (0, 0)),
            pl.BlockSpec((D, width), lambda j: (0, 0)),
        ]
        + ([] if first else [any_spec] * 3),
        out_specs=(
            pl.BlockSpec((3, D), lambda j: (0, 0)),
            row,
            row,
            pl.BlockSpec((LEN, width), lambda j: (item, 0)),
        ),
        input_output_aliases={} if first else {7 + i: 1 + i for i in range(3)},
        compiler_params=params(),
        cost_estimate=cost(2 * LEN * D * width, 20 * LEN * D),
        name="first_back",
    )(mine, other, second, normed, inverse, vectors, outward, *(() if first else held))


def source_kernel(*refs):
    grads, weights, out_ref = refs[:-2], refs[-2], refs[-1]
    width = 3 * LANES
    total = None
    for group, grad_ref in enumerate(grads):
        part = dot_nt(grad_ref[...], weights[:, group * width : (group + 1) * width])
        total = part if total is None else total + part
    out_ref[...] = total.astype(low)


def source_part(grads, inward, item):
    width = 3 * LANES
    groups = len(grads)
    return pl.pallas_call(
        source_kernel,
        out_shape=shape((LEN, D), low),
        grid=(1,),
        in_specs=[pl.BlockSpec((LEN, width), lambda i: (item, 0)) for _ in grads]
        + [pl.BlockSpec((D, groups * width), lambda i: (0, 0))],
        out_specs=pl.BlockSpec((LEN, D), lambda i: (0, 0)),
        compiler_params=params(),
        cost_estimate=cost(2 * LEN * D * width * groups, 2 * (LEN + D) * width * groups),
        name="source",
    )(*grads, inward)


def transpose_into(left_ref, turned_ref):
    for start in range(0, left_ref.shape[0], LEN):
        turned_ref[:, start : start + LEN] = (
            left_ref[start : start + LEN, :].astype(full).T.astype(low)
        )


def weight_grad_kernel(cut_blocks, me_ref, left_ref, right_ref, *refs):
    turned_ref, total_ref = refs[-2:]
    step = pl.program_id(0)

    @pl.when(step == 0)
    def _():
        transpose_into(left_ref, turned_ref)

    if cut_blocks is None:
        refs[0][...] = dot_nn(turned_ref[...], right_ref[...])
        return
    total_ref[...] = dot_nn(turned_ref[...], right_ref[...])
    sent_a, kept_a, sent_b, kept_b = refs[:4]
    rows = sent_a.shape[2]
    layers = sent_a.shape[1]

    def spread(sent, kept, bit):
        for plane in range(4):
            other = plane >> 1 if bit == 0 else plane & 1
            target = sent if (plane >> bit) & 1 else kept
            for k in range(layers):
                start = pl.multiple_of((me_ref[0] ^ (4 * k + plane)) * rows, 8)
                target[other, k] = total_ref[pl.ds(start, rows), :].astype(low)

    @pl.when(step < cut_blocks)
    def _():
        spread(sent_a, kept_a, 0)

    @pl.when(step >= cut_blocks)
    def _():
        spread(sent_b, kept_b, 1)


def weight_grad(left, right, me, size):
    tokens, width = right.shape
    block = 256 if width % 512 == 0 else LANES
    layers, rows = size // 4, D // size
    cut = split_columns(width)
    fast = me is not None
    cut_blocks = cut // block if fast else None
    last = width // block - 1
    if fast:
        piece = (2, layers, rows)

        def spec_a():
            return pl.BlockSpec(
                piece + (block,), lambda j, m: (0, 0, 0, jnp.minimum(j, cut_blocks - 1))
            )

        def spec_b():
            return pl.BlockSpec(
                piece + (block,), lambda j, m: (0, 0, 0, jnp.maximum(j - cut_blocks, 0))
            )

        outs = (
            shape(piece + (cut,), low),
            shape(piece + (cut,), low),
            shape(piece + (width - cut,), low),
            shape(piece + (width - cut,), low),
        )
        out_specs = (spec_a(), spec_a(), spec_b(), spec_b())
    else:
        outs = (shape((D, width), full),)
        out_specs = (pl.BlockSpec((D, block), lambda j, m: (0, j)),)
        me = jnp.zeros((1,), jnp.int32)
    return pl.pallas_call(
        partial(weight_grad_kernel, cut_blocks),
        out_shape=outs,
        grid_spec=pltpu.PrefetchScalarGridSpec(
            num_scalar_prefetch=1,
            grid=(last + 1,),
            in_specs=[
                pl.BlockSpec((tokens, D), lambda j, m: (0, 0)),
                pl.BlockSpec((tokens, block), lambda j, m: (0, j)),
            ],
            out_specs=out_specs,
            scratch_shapes=[pltpu.VMEM((D, tokens), low), pltpu.VMEM((D, block), full)],
        ),
        compiler_params=params(),
        cost_estimate=cost(2 * tokens * D * width, 2 * (tokens * D + tokens * width + D * width)),
        name="weight_grad",
    )(me, left, right)


def adamw(master, gradient, first_moment, second_moment, step_rate, decay_rate, correct):
    first_new = 0.5 * first_moment + 0.5 * gradient
    second_new = 0.5 * second_moment + 0.5 * gradient * gradient
    moved = first_new / correct / (jnp.sqrt(second_new / correct) + 1e-08)
    return (master - step_rate * (moved + decay_rate * master), first_new, second_new)


def per_device(
    activations,
    cotangent,
    token_weight,
    lengths,
    step_count,
    inward_weight,
    output_weight,
    up_weight,
    down_weight,
    heads_bias,
    hidden_bias,
    norm_vectors,
    *moments,
):
    size = lax.axis_size("dp")
    rows, width = inward_weight.shape[1], inward_weight.shape[2]
    hidden_width = up_weight.shape[1]
    groups = width // LANES
    tokens = activations.shape[0]
    count = tokens // LEN
    fast = size == 16 and rows % 16 == 0
    me = lax.axis_index("dp").astype(jnp.int32).reshape(1) if fast else None

    small = jnp.concatenate(
        [heads_bias.reshape(-1), hidden_bias.reshape(-1), norm_vectors.reshape(-1)]
    )
    per_row = small.shape[0] // rows
    small_block = jnp.pad(small.reshape(rows, per_row), ((0, 0), (0, LANES - per_row)))
    inward_shard = jnp.concatenate(
        [
            inward_weight.reshape(3, rows, groups, LANES)
            .transpose(1, 2, 0, 3)
            .reshape(rows, 3 * width),
            small_block,
        ],
        axis=1,
    ).astype(low)
    outward_shard = output_weight.T.astype(low)
    upward_shard = up_weight.astype(low)
    downward_shard = down_weight.T.astype(low)
    shards = (inward_shard, outward_shard, upward_shard, downward_shard)

    if fast:
        gathered = []
        gate = None
        for shard in shards:
            if gate is not None:
                shard = after(shard, *gate)
            found = gather_planes(shard, size)
            gate = found[1:]
            gathered.append(place(gather_pieces(found, size), me))
    else:
        gathered = [lax.all_gather(shard, "dp", axis=0, tiled=True) for shard in shards]
    inward, outward, upward, downward = gathered

    smalls = inward[:, 3 * width : 3 * width + per_row].astype(full).reshape(size, -1)
    heads_size, hidden_size = heads_bias.size, hidden_bias.size
    head_biases = (
        smalls[:, :heads_size].reshape(size, 2, -1).transpose(1, 2, 0).reshape(2, width)
    )
    hidden_biases = smalls[:, heads_size : heads_size + hidden_size].T.reshape(1, hidden_width)
    vectors = (
        smalls[:, heads_size + hidden_size :].reshape(size, 6, rows).transpose(1, 0, 2)
    ).reshape(6, D)

    live = lax.broadcasted_iota(jnp.int32, (count, LEN), 1) < lengths[:, None]
    scale = (token_weight.reshape(count, LEN) * live.astype(jnp.int32)).astype(full)
    scale = scale.reshape(tokens, 1)

    qkv, weights, context = attend(lengths, activations, inward, head_biases)
    mine = [outward_part(context, outward, item) for item in range(count)]
    other = [swap_cores(part) for part in mine]
    held = None
    mine_down = []
    for item in range(count):
        part, *held = expand(
            mine[item], other[item], activations, vectors, hidden_biases, upward, downward,
            held, item,
        )
        mine_down.append(part)
    active, slope, middle, normed, inverse = held
    other_down = [swap_cores(part) for part in mine_down]
    held = None
    mine_middle, second_sums, hidden_sums = [], [], []
    for item in range(count):
        part, sums, hidden_sum, *held = contract(
            mine_down[item], other_down[item], normed, cotangent, scale, vectors, slope,
            upward, downward, held, item,
        )
        mine_middle.append(part)
        second_sums.append(sums)
        hidden_sums.append(hidden_sum)
    output_rows, second_grad, second_low, hidden_grad = held
    other_middle = [swap_cores(part) for part in mine_middle]

    def reduced(left, right):
        pieces = weight_grad(left, right, me, size)
        if not fast:
            return lax.psum_scatter(pieces[0], "dp", scatter_dimension=0, tiled=True)
        state = reduce_last(reduce_middle(reduce_start(pieces, size), size), size)
        return reduce_sum(state)

    downward_grad = reduced(second_low, active)
    upward_grad = reduced(middle, hidden_grad)
    held = None
    first_sums = []
    for item in range(count):
        sums, *held = first_back(
            mine_middle[item], other_middle[item], second_grad, normed, inverse, vectors,
            outward, held, item,
        )
        first_sums.append(sums)
    first_grad, first_low, context_grad = held
    outward_grad = reduced(first_low, context)
    stacked, head_sums, inward_grads = [], [], []
    for group in range(groups):
        grads, sums = attend_back(qkv, weights, context_grad, group)
        stacked.append(grads)
        head_sums.append(sums)
        inward_grads.append(reduced(activations, grads))
    mine_source = [source_part(stacked, inward, item) for item in range(count)]
    other_source = [swap_cores(part) for part in mine_source]
    input_grad = (
        jnp.concatenate(
            [a.astype(full) + b.astype(full) for a, b in zip(mine_source, other_source)]
        )
        + first_grad
    )

    head_grad = jnp.concatenate(head_sums, axis=1)
    norm_grad = jnp.concatenate([sum(first_sums), sum(second_sums)])
    outgoing = jnp.concatenate(
        [
            head_grad.reshape(2, -1, size).transpose(2, 0, 1).reshape(size, -1),
            sum(hidden_sums).reshape(-1, size).T,
            norm_grad.reshape(6, size, rows).transpose(1, 0, 2).reshape(size, -1),
        ],
        axis=1,
    )
    if fast:
        order = lax.iota(jnp.int32, size) ^ me
        onehot = (order[:, None] == lax.iota(jnp.int32, size)[None, :]).astype(full)
        turned = jnp.dot(onehot, outgoing, precision=lax.Precision.HIGHEST)
        turned = turned.reshape(size // 4, 2, 2, -1)
        kept = turned[:, :, 0] + hop(turned[:, :, 1], 1, size)
        kept = kept[:, 0] + hop(kept[:, 1], 2, size)
        small_grad = kept[0]
        for k in range(1, size // 4):
            small_grad = small_grad + hop(kept[k], 4 * k, size)
    else:
        small_grad = lax.psum_scatter(outgoing, "dp", scatter_dimension=0, tiled=True)
    small_grad = small_grad.reshape(-1)

    inward_grad = jnp.stack(
        [
            jnp.concatenate(
                [grad[:, kind * LANES : (kind + 1) * LANES] for grad in inward_grads], axis=1
            )
            for kind in range(3)
        ]
    )
    grads = (
        inward_grad,
        outward_grad.T,
        upward_grad,
        downward_grad.T,
        small_grad[:heads_size].reshape(heads_bias.shape),
        small_grad[heads_size : heads_size + hidden_size].reshape(hidden_bias.shape),
        small_grad[heads_size + hidden_size :].reshape(norm_vectors.shape),
    )

    step_value = step_count[0].astype(full)
    correct = 1.0 - jnp.power(0.5, step_value)
    plan = (step_value + 4.0) / 12.0
    rates = (D ** (-0.5), (6 * D // LEN) ** (-0.5), D ** (-0.5), FF ** (-0.5), 0.5, 0.5, 0.3)
    decays = (0.01, 0.01, 0.01, 0.01, 0.0, 0.0, 0.0)
    masters = (
        inward_weight,
        output_weight,
        up_weight,
        down_weight,
        heads_bias,
        hidden_bias,
        norm_vectors,
    )
    results = [output_rows, input_grad]
    for at in range(7):
        results.extend(
            adamw(
                masters[at],
                grads[at],
                moments[at],
                moments[7 + at],
                rates[at] * plan,
                decays[at],
                correct,
            )
        )
    return tuple(results)


def solution(mesh):
    matrices = (
        P(None, "dp", "tensor"),
        P("tensor", "dp"),
        P("dp", "tensor"),
        P("tensor", "dp"),
        P(None, "tensor", "dp"),
        P("tensor", "dp"),
        P(None, "dp"),
    )
    in_specs = (
        (P("dp", None), P("dp", None), P("dp"), P("dp"), P()) + matrices + matrices + matrices
    )
    out_specs = (P("dp", None), P("dp", None)) + tuple(
        spec for spec in matrices for _ in range(3)
    )
    return jax.shard_map(
        per_device, mesh=mesh, in_specs=in_specs, out_specs=out_specs, check_vma=False
    )
```

time: 1220 us -> 433 us (0.35)
  waiting for transfers between devices: 572 us -> 76.4 us
  blocking collectives: 235 us -> 0 us
  matrix products: 201 us -> 0.21 us
  Pallas kernels: 0 us -> 194 us
  starting transfers between devices: 0.5 us -> 108 us
  local copies, waits for them, and re-layouts: 114 us -> 18.6 us
  other arithmetic: 70.8 us -> 27.4 us
  between operations: 16.7 us -> 3.35 us
    reduce_scatter x3 -> x0, waiting for transfers between devices: 282 us -> none  [the longest x1 141 us: per_device(): lax.psum_scatter(upward_grad, 'dp', scatter_dimension=0, tiled=True)]
    pallas_call x0 -> x29, Pallas kernels: none -> 194 us  [the longest x6 43.3 us: weight_grad(): pl.pallas_call(partial(weight_grad_kernel, cut_blocks), out_shape=outs, g...]
    unnamed x14 -> x0, waiting for transfers between devices: 180 us -> none
    dot_general x31 -> x1, matrix products: 163 us -> 0.21 us  [per_device(): turned = jnp.dot(onehot, outgoing, precision=lax.Precision.HIGHEST)]
    all_gather x4 -> x0, blocking collectives: 158 us -> none  [the longest x1 42.4 us: per_device(): lax.all_gather(heads_bias.astype(jnp.bfloat16), 'dp', axis=2, tiled=True)]
    ppermute x0 -> x95, starting transfers between devices: none -> 108 us  [the longest x83 106 us: hop(): return lax.ppermute(value, 'dp', [(d, d ^ offset) for d in range(size)])]
    unnamed x1 -> x0, blocking collectives: 77.4 us -> none
    ppermute x0 -> x95, waiting for transfers between devices: none -> 76.4 us  [the longest x83 76.3 us: hop(): return lax.ppermute(value, 'dp', [(d, d ^ offset) for d in range(size)])]
  transfers between devices with their start and end apart: 12 -> 95, of which waited for: 8 -> 35; matrix products, arithmetic and copies ran while one was open for 18% -> 7% of each run, Pallas kernels for 0% -> 45%
where the time goes in v1:
time: 433 us; the launch traced here: 428 us
  Pallas kernels  194 us (45%)
  starting transfers between devices  108 us (25%)
  waiting for transfers between devices  76.4 us (18%)
  other arithmetic  27.4 us (6%)
  local copies, waits for them, and re-layouts  18.6 us (4%)
    ppermute x83, starting transfers between devices, hop(): return lax.ppermute(value, 'dp', [(d, d ^ offset) for d in range(size)])  106 us
    ppermute x83, waiting for transfers between devices, hop(): return lax.ppermute(value, 'dp', [(d, d ^ offset) for d in range(size)])  76.3 us
    pallas_call x6, Pallas kernels, weight_grad(): pl.pallas_call(partial(weight_grad_kernel, cut_blocks), out_shape=outs, g...  43.3 us
    pallas_call x3, Pallas kernels, contract(): pl.pallas_call(kernel, out_shape=outs, grid=(hidden // block,), in_specs=...  32.6 us
    pallas_call x3, Pallas kernels, expand(): pl.pallas_call(kernel, out_shape=outs, grid=(hidden // block,), in_specs=...  29.7 us
    pallas_call x1, Pallas kernels, attend(): pl.pallas_call(attend_kernel, out_shape=(shape((rows, groups * width), lo...  20.7 us
    pallas_call x3, Pallas kernels, attend_back(): pl.pallas_call(attend_back_kernel, out_shape=(shape((rows, width), low),...  20 us
    pallas_call x3, Pallas kernels, first_back(): pl.pallas_call(kernel, out_shape=(shape((3, D), full), shape((rows, D), f...  15.9 us
  transfers between devices with their start and end apart: 95, of which 35 were waited for; matrix products, arithmetic and copies ran while one was open for 7% of the time, Pallas kernels for 45%

profile of v1, /device:TPU:0, one launch (start us, length us, event | category | flops | bytes accessed | tf_op | source)
XLA Modules:
  0.0 428.3 jit_solution(15658213493274280085)
XLA Ops:
  5.5 3.1 collective-permute-start
  8.7 2.6 collective-permute-start.1
  13.4 7.6 %collective-permute-done.1 = bf16[48,1280]{1,0:T(8,128)(2,1)S(1)} collective-permute-done((bf16[48,1280]{1,0:T(8,128)(2,1)S(1)}, bf16[48,1280]{1,0:T(8,128)(2,1)S(1)}, u32[]{:S(2)}, u32[]{:S(2)}) %collective-permute-start.1) | collective-permute-done | bytes 122912 | tf_op jit(solution)/shard_map/ppermute | solution.py:67
  25.4 2.9 collective-permute-done.10
  37.4 2.7 collective-permute-done.15.refs_5_
  49.6 2.5 collective-permute-start.30
  54.3 5.6 %collective-permute-done.29 = bf16[48,1536]{1,0:T(8,128)(2,1)S(1)} collective-permute-done((bf16[48,1536]{1,0:T(8,128)(2,1)S(1)}, bf16[48,1536]{1,0:T(8,128)(2,1)S(1)}, u32[]{:S(2)}, u32[]{:S(2)}) %collective-permute-start.29) | collective-permute-done | bytes 147488 | tf_op jit(solution)/shard_map/ppermute | solution.py:67
  64.6 3.9 collective-permute-done.7.refs_6_
  69.4 7.0 %collective-permute-done.5.refs_3_ = bf16[4,48,640]{2,1,0:T(8,128)(2,1)S(1)} collective-permute-done((bf16[4,48,640]{2,1,0:T(8,128)(2,1)S(1)}, bf16[4,48,640]{2,1,0:T(8,128)(2,1)S(1)}, u32[]{:S(2)}, u32[]{:S(2)}) %collective-permute-start.5) | collective-permute-done | bytes 245792 | tf_op jit(solution)/shard_map/ppermute | solution.py:67
  78.4 3.1 place.4.w_ref.refs_3_
  83.4 3.8 collective-permute-start.31
  87.3 20.7 %attend.1 = (bf16[1536,1152]{1,0:T(8,128)(2,1)}, bf16[9,2,512,512]{3,2,1,0:T(8,128)(2,1)}, bf16[1536,384]{1,0:T(8,128)(2,1)}) custom-call(s32[3]{0:T(128)} %length_ref.1, bf16[1536,768]{1,0:T(8,128)(2,1)} %left_ref.5, bf16[768,1280]{1,0:T(8,128)(2,1)} %place.4.w_ref.refs_3_, f32[2,384]{1,0:T(2,128)} %reshape.298.bias_ref), custom_call_target="tpu_custom_call" | custom-call | flops 5133828096 | bytes 9437184 | tf_op jit(solution)/shard_map/attend/pallas_call | solution.py:192
  108.0 2.7 outward.5.refs_0_
  114.9 2.7 outward.4.mine_ref
  117.6 2.7 outward.3.mine_ref
  122.9 3.7 collective-permute-done.27.refs_7_
  129.3 3.2 place.6.refs_5_.up_ref.refs_7_
  132.5 2.9 collective-permute-done.36.refs_7_
  136.1 3.1 place.7.refs_6_.down_ref.refs_8_
  139.2 9.7 %expand.3 = (bf16[512,768]{1,0:T(8,128)(2,1)}, bf16[1536,1536]{1,0:T(8,128)(2,1)}, bf16[1536,1536]{1,0:T(8,128)(2,1)}, bf16[1536,768]{1,0:T(8,128)(2,1)}, f32[1536,768]{1,0:T(8,128)}, /*index=5*/f32[1536,1]{1,0:T(8,128)}) custom-call(bf16[512,768]{1,0:T(8,128)(2,1)} %outward.5.refs_0_, bf16[512,768]{1,0:T(8,128)(2,1)} %collective-permute-done.38.refs_1_, ...), custom_call_target="tpu_custom_call" | custom-call | flops 2415919104 | bytes 7864320 | tf_op jit(solution)/shard_map/expand/pallas_call | solution.py:371
  149.9 9.7 %expand.4 = (bf16[512,768]{1,0:T(8,128)(2,1)}, bf16[1536,1536]{1,0:T(8,128)(2,1)}, bf16[1536,1536]{1,0:T(8,128)(2,1)}, bf16[1536,768]{1,0:T(8,128)(2,1)}, f32[1536,768]{1,0:T(8,128)}, /*index=5*/f32[1536,1]{1,0:T(8,128)}) custom-call(bf16[512,768]{1,0:T(8,128)(2,1)} %outward.4.mine_ref, ...), custom_call_target="tpu_custom_call", output_to_operand_aliasing={{1}: (7, {}), {2}: (8, {}), {3}: (9, {}), {4}: (10, {}), {5... | custom-call | flops 2415919104 | bytes 7864320 | tf_op jit(solution)/shard_map/expand/pallas_call | solution.py:371
  161.1 10.2 %expand.5 = (bf16[512,768]{1,0:T(8,128)(2,1)}, bf16[1536,1536]{1,0:T(8,128)(2,1)}, bf16[1536,1536]{1,0:T(8,128)(2,1)}, bf16[1536,768]{1,0:T(8,128)(2,1)}, f32[1536,768]{1,0:T(8,128)}, /*index=5*/f32[1536,1]{1,0:T(8,128)}) custom-call(bf16[512,768]{1,0:T(8,128)(2,1)} %outward.3.mine_ref, ...), custom_call_target="tpu_custom_call", output_to_operand_aliasing={{1}: (7, {}), {2}: (8, {}), {3}: (9, {}), {4}: (10, {}), {5... | custom-call | flops 2415919104 | bytes 7864320 | tf_op jit(solution)/shard_map/expand/pallas_call | solution.py:371
  174.2 10.8 %contract.3 = (bf16[512,768]{1,0:T(8,128)(2,1)}, f32[3,768]{1,0:T(4,128)}, f32[1,1536]{1,0:T(1,128)}, bf16[1536,768]{1,0:T(8,128)(2,1)}, f32[1536,768]{1,0:T(8,1...) custom-call(bf16[512,768]{1,0:T(8,128)(2,1)} %get-tuple-element.174.refs_0_, bf16[512,768]{1,0:T(8,128)(2,1)} %copy-done.16, ...), custom_call_target="tpu_custom_call" | custom-call | flops 2415919104 | bytes 7864320 | tf_op jit(solution)/shard_map/contract/pallas_call | solution.py:460
  186.5 10.8 %contract.4 = (bf16[512,768]{1,0:T(8,128)(2,1)}, f32[3,768]{1,0:T(4,128)}, f32[1,1536]{1,0:T(1,128)}, bf16[1536,768]{1,0:T(8,128)(2,1)}, f32[1536,768]{1,0:T(8,1...) custom-call(bf16[512,768]{1,0:T(8,128)(2,1)} %get-tuple-element.173., ...), custom_call_target="tpu_custom_call", output_to_operand_aliasing={{3}: (9, {}), {4}: (10, {}), {5}: (11, {}), {6}: (12, {})} | custom-call | flops 2415919104 | bytes 7864320 | tf_op jit(solution)/shard_map/contract/pallas_call | solution.py:460
  198.3 10.9 %contract.5 = (bf16[512,768]{1,0:T(8,128)(2,1)}, f32[3,768]{1,0:T(4,128)}, f32[1,1536]{1,0:T(1,128)}, bf16[1536,768]{1,0:T(8,128)(2,1)}, f32[1536,768]{1,0:T(8,1...) custom-call(bf16[512,768]{1,0:T(8,128)(2,1)} %get-tuple-element.170., ...), custom_call_target="tpu_custom_call", output_to_operand_aliasing={{3}: (9, {}), {4}: (10, {}), {5}: (11, {}), {6}: (12, {})} | custom-call | flops 2415919104 | bytes 7864320 | tf_op jit(solution)/shard_map/contract/pallas_call | solution.py:460
  209.2 9.6 %weight_grad.11 = (bf16[2,4,48,768]{3,2,1,0:T(8,128)(2,1)}, bf16[2,4,48,768]{3,2,1,0:T(8,128)(2,1)}, bf16[2,4,48,768]{3,2,1,0:T(8,128)(2,1)}, bf16[2,4,48,768]{3,2,1,0:T(8,128)(2,1)}) custom-call(s32[1]{0:T(128)} %bitcast.me_ref, bf16[1536,768]{1,0:T(8,128)(2,1)} %get-tuple-element.250.left_ref, bf16[1536,1536]{1,0:T(8,128)(2,1)} %get-tuple-element.251.right_ref), custom_call_target="tpu_custom_call" | custom-call | flops 3623878656 | bytes 9437184 | tf_op jit(solution)/shard_map/weight_grad/pallas_call | solution.py:650
  221.6 9.7 %weight_grad.10 = (bf16[2,4,48,768]{3,2,1,0:T(8,128)(2,1)}, bf16[2,4,48,768]{3,2,1,0:T(8,128)(2,1)}, bf16[2,4,48,768]{3,2,1,0:T(8,128)(2,1)}, bf16[2,4,48,768]{3,2,1,0:T(8,128)(2,1)}) custom-call(s32[1]{0:T(128)} %bitcast.me_ref, bf16[1536,768]{1,0:T(8,128)(2,1)} %get-tuple-element.239.left_ref, bf16[1536,1536]{1,0:T(8,128)(2,1)} %get-tuple-element.240.right_ref), custom_call_target="tpu_custom_call" | custom-call | flops 3623878656 | bytes 9437184 | tf_op jit(solution)/shard_map/weight_grad/pallas_call | solution.py:650
  240.8 6.5 %collective-permute-done.77 = bf16[2,4,48,768]{3,2,1,0:T(8,128)(2,1)S(1)} collective-permute-done((bf16[2,4,48,768]{3,2,1,0:T(8,128)(2,1)}, bf16[2,4,48,768]{3,2,1,0:T(8,128)(2,1)S(1)}, u32[]{:S(2)}, u32[]{:S(2)}) %collective-permute-start.77) | collective-permute-done | bytes 589856 | tf_op jit(solution)/shard_map/ppermute | solution.py:67
  253.5 5.3 %first_back.3 = (f32[3,768]{1,0:T(4,128)}, f32[1536,768]{1,0:T(8,128)}, bf16[1536,768]{1,0:T(8,128)(2,1)}, bf16[1536,384]{1,0:T(8,128)(2,1)}) custom-call(bf16[512,768]{1,0:T(8,128)(2,1)} %get-tuple-element.190.refs_0_, bf16[512,768]{1,0:T(8,128)(2,1)} %copy-done.18, f32[1536,768]{1,0:T(8,128)} %get-tuple-element.187.refs_2_.second_ref, ...), custom_call_target="tpu_custom_call" | custom-call | flops 301989888 | bytes 7864320 | tf_op jit(solution)/shard_map/first_back/pallas_call | solution.py:520
  259.7 5.3 %first_back.4 = (f32[3,768]{1,0:T(4,128)}, f32[1536,768]{1,0:T(8,128)}, bf16[1536,768]{1,0:T(8,128)(2,1)}, bf16[1536,384]{1,0:T(8,128)(2,1)}) custom-call(bf16[512,768]{1,0:T(8,128)(2,1)} %get-tuple-element.189.mine_ref, bf16[512,768]{1,0:T(8,128)(2,1)} %copy-done.13, ...), custom_call_target="tpu_custom_call", output_to_operand_aliasing={{1}: (7, {}), {2}: (8, {}), {3}: (9, {})} | custom-call | flops 301989888 | bytes 7864320 | tf_op jit(solution)/shard_map/first_back/pallas_call | solution.py:520
  265.9 5.3 %first_back.5 = (f32[3,768]{1,0:T(4,128)}, f32[1536,768]{1,0:T(8,128)}, bf16[1536,768]{1,0:T(8,128)(2,1)}, bf16[1536,384]{1,0:T(8,128)(2,1)}) custom-call(bf16[512,768]{1,0:T(8,128)(2,1)} %get-tuple-element.186.mine_ref, bf16[512,768]{1,0:T(8,128)(2,1)} %copy-done.17, ...), custom_call_target="tpu_custom_call", output_to_operand_aliasing={{1}: (7, {}), {2}: (8, {}), {3}: (9, {})} | custom-call | flops 301989888 | bytes 7864320 | tf_op jit(solution)/shard_map/first_back/pallas_call | solution.py:520
  271.2 6.8 %attend_back.5 = (bf16[1536,384]{1,0:T(8,128)(2,1)}, f32[2,128]{1,0:T(2,128)}) custom-call(bf16[1536,1152]{1,0:T(8,128)(2,1)} %get-tuple-element.184.qkv_ref, bf16[9,2,512,512]{3,2,1,0:T(8,128)(2,1)} %get-tuple-element.185.weight_ref, bf16[1536,384]{1,0:T(8,128)(2,1)} %get-tuple-element.197.grad_ref), custom_call_target="tpu_custom_call" | custom-call | flops 1610612736 | bytes 5505024 | tf_op jit(solution)/shard_map/attend_back/pallas_call | solution.py:263
  278.0 6.6 %attend_back.4 = (bf16[1536,384]{1,0:T(8,128)(2,1)}, f32[2,128]{1,0:T(2,128)}) custom-call(bf16[1536,1152]{1,0:T(8,128)(2,1)} %get-tuple-element.184.qkv_ref, bf16[9,2,512,512]{3,2,1,0:T(8,128)(2,1)} %get-tuple-element.185.weight_ref, bf16[1536,384]{1,0:T(8,128)(2,1)} %get-tuple-element.197.grad_ref), custom_call_target="tpu_custom_call" | custom-call | flops 1610612736 | bytes 5505024 | tf_op jit(solution)/shard_map/attend_back/pallas_call | solution.py:263
  284.6 6.6 %attend_back.3 = (bf16[1536,384]{1,0:T(8,128)(2,1)}, f32[2,128]{1,0:T(2,128)}) custom-call(bf16[1536,1152]{1,0:T(8,128)(2,1)} %get-tuple-element.184.qkv_ref, bf16[9,2,512,512]{3,2,1,0:T(8,128)(2,1)} %get-tuple-element.185.weight_ref, bf16[1536,384]{1,0:T(8,128)(2,1)} %get-tuple-element.197.grad_ref), custom_call_target="tpu_custom_call" | custom-call | flops 1610612736 | bytes 5505024 | tf_op jit(solution)/shard_map/attend_back/pallas_call | solution.py:263
  291.2 5.9 %weight_grad.6 = (bf16[2,4,48,256]{3,2,1,0:T(8,128)(2,1)}, bf16[2,4,48,256]{3,2,1,0:T(8,128)(2,1)}, bf16[2,4,48,128]{3,2,1,0:T(8,128)(2,1)}, bf16[2,4,48,128]{3,2,1,0:T(8,128)(2,1)}) custom-call(s32[1]{0:T(128)} %bitcast.me_ref, bf16[1536,768]{1,0:T(8,128)(2,1)} %left_ref.5, bf16[1536,384]{1,0:T(8,128)(2,1)} %get-tuple-element.198.refs_0_.right_ref), custom_call_target="tpu_custom_call" | custom-call | flops 905969664 | bytes 4128768 | tf_op jit(solution)/shard_map/weight_grad/pallas_call | solution.py:650
  297.1 5.9 %weight_grad.7 = (bf16[2,4,48,256]{3,2,1,0:T(8,128)(2,1)}, bf16[2,4,48,256]{3,2,1,0:T(8,128)(2,1)}, bf16[2,4,48,128]{3,2,1,0:T(8,128)(2,1)}, bf16[2,4,48,128]{3,2,1,0:T(8,128)(2,1)}) custom-call(s32[1]{0:T(128)} %bitcast.me_ref, bf16[1536,768]{1,0:T(8,128)(2,1)} %left_ref.5, bf16[1536,384]{1,0:T(8,128)(2,1)} %get-tuple-element.199.refs_1_.right_ref), custom_call_target="tpu_custom_call" | custom-call | flops 905969664 | bytes 4128768 | tf_op jit(solution)/shard_map/weight_grad/pallas_call | solution.py:650
  303.0 5.9 %weight_grad.8 = (bf16[2,4,48,256]{3,2,1,0:T(8,128)(2,1)}, bf16[2,4,48,256]{3,2,1,0:T(8,128)(2,1)}, bf16[2,4,48,128]{3,2,1,0:T(8,128)(2,1)}, bf16[2,4,48,128]{3,2,1,0:T(8,128)(2,1)}) custom-call(s32[1]{0:T(128)} %bitcast.me_ref, bf16[1536,768]{1,0:T(8,128)(2,1)} %left_ref.5, bf16[1536,384]{1,0:T(8,128)(2,1)} %get-tuple-element.200.refs_2_.right_ref), custom_call_target="tpu_custom_call" | custom-call | flops 905969664 | bytes 4128768 | tf_op jit(solution)/shard_map/weight_grad/pallas_call | solution.py:650
  309.0 4.2 source.3
  314.2 4.1 source.4
  319.6 4.1 source.5
  323.9 2.4 collective-permute-start.93
  328.2 6.2 %weight_grad.9 = (bf16[2,4,48,256]{3,2,1,0:T(8,128)(2,1)}, bf16[2,4,48,256]{3,2,1,0:T(8,128)(2,1)}, bf16[2,4,48,128]{3,2,1,0:T(8,128)(2,1)}, bf16[2,4,48,128]{3,2,1,0:T(8,128)(2,1)}) custom-call(s32[1]{0:T(128)} %bitcast.me_ref, bf16[1536,768]{1,0:T(8,128)(2,1)} %get-tuple-element.229.left_ref, bf16[1536,384]{1,0:T(8,128)(2,1)} %get-tuple-element.150.context_ref.right_ref), custom_call_target="tpu_custom_call" | custom-call | flops 905969664 | bytes 4128768 | tf_op jit(solution)/shard_map/weight_grad/pallas_call | solution.py:650
  362.5 2.4 collective-permute-done.72
  375.0 2.4 collective-permute-done.65
  379.4 2.5 collective-permute-start.81
  381.9 4.1 collective-permute-done.89
  420.8 2.7 collective-permute-done.75
  425.3 2.8 maximum_add_fusion
  (513 shorter events, 158.9 us)
Async XLA Ops:
  8.7 12.3 %collective-permute-start.1 = (bf16[48,1280]{1,0:T(8,128)(2,1)S(1)}, bf16[48,1280]{1,0:T(8,128)(2,1)S(1)}, u32[]{:S(2)}, u32[]{:S(2)}) collective-permute-start(bf16[48,1280]{1,0:T(8,128)(2,1)S(1)} %pad_maximum_fusion.11), channel_id=1, source_target_pairs={{0,16},{2,18},{4,20},{6,22},{8,24},{10,26},{12,28},{14,30},{16,0},... | collective-permute-start | bytes 368648 | tf_op jit(solution)/shard_map/ppermute | solution.py:67
  29.7 12.3 %collective-permute-start.19 = (bf16[48,1536]{1,0:T(8,128)(2,1)S(1)}, bf16[48,1536]{1,0:T(8,128)(2,1)S(1)}, u32[]{:S(2)}, u32[]{:S(2)}) collective-permute-start(bf16[48,1536]{1,0:T(8,128)(2,1)S(1)} %convert_element_type.389), channel_id=1, source_target_pairs={{0,8},{2,10},{4,12},{6,14},{8,0},{10,2},{12,4},{14,6},{16,24},{18,... | collective-permute-start | bytes 442376 | tf_op jit(solution)/shard_map/ppermute | solution.py:67
  30.0 13.6 %collective-permute-start.20 = (bf16[48,1536]{1,0:T(8,128)(2,1)S(1)}, bf16[48,1536]{1,0:T(8,128)(2,1)S(1)}, u32[]{:S(2)}, u32[]{:S(2)}) collective-permute-start(bf16[48,1536]{1,0:T(8,128)(2,1)S(1)} %convert_element_type.389), channel_id=1, source_target_pairs={{0,16},{2,18},{4,20},{6,22},{8,24},{10,26},{12,28},{14,30},{16,0},... | collective-permute-start | bytes 442376 | tf_op jit(solution)/shard_map/ppermute | solution.py:67
  31.8 12.3 %collective-permute-start.21 = (bf16[48,1536]{1,0:T(8,128)(2,1)S(1)}, bf16[48,1536]{1,0:T(8,128)(2,1)S(1)}, u32[]{:S(2)}, u32[]{:S(2)}) collective-permute-start(bf16[48,1536]{1,0:T(8,128)(2,1)S(1)} %convert_element_type.389), channel_id=1, source_target_pairs={{0,24},{2,26},{4,28},{6,30},{8,16},{10,18},{12,20},{14,22},{16,8},... | collective-permute-start | bytes 442376 | tf_op jit(solution)/shard_map/ppermute | solution.py:67
  46.1 15.9 %collective-permute-start.4 = (bf16[4,48,640]{2,1,0:T(8,128)(2,1)S(1)}, bf16[4,48,640]{2,1,0:T(8,128)(2,1)S(1)}, u32[]{:S(2)}, u32[]{:S(2)}) collective-permute-start(bf16[4,48,640]{2,1,0:T(8,128)(2,1)S(1)} %get-tuple-element.148.refs_0_), channel_id=1, source_target_pairs={{0,4},{2,6},{4,0},{6,2},{8,12},{10,14},{12,8},{14,10},{16,20},{18,... | collective-permute-start | bytes 737288 | tf_op jit(solution)/shard_map/ppermute | solution.py:67
  47.2 16.9 %collective-permute-start.3 = (bf16[4,48,640]{2,1,0:T(8,128)(2,1)S(1)}, bf16[4,48,640]{2,1,0:T(8,128)(2,1)S(1)}, u32[]{:S(2)}, u32[]{:S(2)}) collective-permute-start(bf16[4,48,640]{2,1,0:T(8,128)(2,1)S(1)} %get-tuple-element.148.refs_0_), channel_id=1, source_target_pairs={{0,2},{2,0},{4,6},{6,4},{8,10},{10,8},{12,14},{14,12},{16,18},{18,... | collective-permute-start | bytes 737288 | tf_op jit(solution)/shard_map/ppermute | solution.py:67
  47.8 15.0 %collective-permute-start.6 = (bf16[4,48,640]{2,1,0:T(8,128)(2,1)S(1)}, bf16[4,48,640]{2,1,0:T(8,128)(2,1)S(1)}, u32[]{:S(2)}, u32[]{:S(2)}) collective-permute-start(bf16[4,48,640]{2,1,0:T(8,128)(2,1)S(1)} %get-tuple-element.149.refs_4_), channel_id=1, source_target_pairs={{0,2},{2,0},{4,6},{6,4},{8,10},{10,8},{12,14},{14,12},{16,18},{18,... | collective-permute-start | bytes 737288 | tf_op jit(solution)/shard_map/ppermute | solution.py:67
  49.2 10.6 %collective-permute-start.29 = (bf16[48,1536]{1,0:T(8,128)(2,1)S(1)}, bf16[48,1536]{1,0:T(8,128)(2,1)S(1)}, u32[]{:S(2)}, u32[]{:S(2)}) collective-permute-start(bf16[48,1536]{1,0:T(8,128)(2,1)S(1)} %convert_bitcast_fusion), channel_id=1, source_target_pairs={{0,16},{2,18},{4,20},{6,22},{8,24},{10,26},{12,28},{14,30},{16,0},... | collective-permute-start | bytes 442376 | tf_op jit(solution)/shard_map/ppermute | solution.py:67
  49.6 10.7 %collective-permute-start.30 = (bf16[48,1536]{1,0:T(8,128)(2,1)S(1)}, bf16[48,1536]{1,0:T(8,128)(2,1)S(1)}, u32[]{:S(2)}, u32[]{:S(2)}) collective-permute-start(bf16[48,1536]{1,0:T(8,128)(2,1)S(1)} %convert_bitcast_fusion), channel_id=1, source_target_pairs={{0,24},{2,26},{4,28},{6,30},{8,16},{10,18},{12,20},{14,22},{16,8},... | collective-permute-start | bytes 442376 | tf_op jit(solution)/shard_map/ppermute | solution.py:67
  60.3 23.2 %collective-permute-start.23 = (bf16[4,48,768]{2,1,0:T(8,128)(2,1)S(1)}, bf16[4,48,768]{2,1,0:T(8,128)(2,1)S(1)}, u32[]{:S(2)}, u32[]{:S(2)}) collective-permute-start(bf16[4,48,768]{2,1,0:T(8,128)(2,1)S(1)} %get-tuple-element.155.refs_0_), channel_id=1, source_target_pairs={{0,4},{2,6},{4,0},{6,2},{8,12},{10,14},{12,8},{14,10},{16,20},{18,... | collective-permute-start | bytes 884744 | tf_op jit(solution)/shard_map/ppermute | solution.py:67
  62.0 25.2 %collective-permute-start.25 = (bf16[4,48,768]{2,1,0:T(8,128)(2,1)S(1)}, bf16[4,48,768]{2,1,0:T(8,128)(2,1)S(1)}, u32[]{:S(2)}, u32[]{:S(2)}) collective-permute-start(bf16[4,48,768]{2,1,0:T(8,128)(2,1)S(1)} %get-tuple-element.156.refs_4_), channel_id=1, source_target_pairs={{0,2},{2,0},{4,6},{6,4},{8,10},{10,8},{12,14},{14,12},{16,18},{18,... | collective-permute-start | bytes 884744 | tf_op jit(solution)/shard_map/ppermute | solution.py:67
  62.8 13.6 %collective-permute-start.5 = (bf16[4,48,640]{2,1,0:T(8,128)(2,1)S(1)}, bf16[4,48,640]{2,1,0:T(8,128)(2,1)S(1)}, u32[]{:S(2)}, u32[]{:S(2)}) collective-permute-start(bf16[4,48,640]{2,1,0:T(8,128)(2,1)S(1)} %collective-permute-done.4.refs_2_), channel_id=1, source_target_pairs={{0,2},{2,0},{4,6},{6,4},{8,10},{10,8},{12,14},{14,12},{16,18},{18,... | collective-permute-start | bytes 737288 | tf_op jit(solution)/shard_map/ppermute | solution.py:67
  64.1 12.5 %collective-permute-start.8 = (bf16[4,48,640]{2,1,0:T(8,128)(2,1)S(1)}, bf16[4,48,640]{2,1,0:T(8,128)(2,1)S(1)}, u32[]{:S(2)}, u32[]{:S(2)}) collective-permute-start(bf16[4,48,640]{2,1,0:T(8,128)(2,1)S(1)} %collective-permute-done.6.refs_5_), channel_id=1, source_target_pairs={{0,4},{2,6},{4,0},{6,2},{8,12},{10,14},{12,8},{14,10},{16,20},{18,... | collective-permute-start | bytes 737288 | tf_op jit(solution)/shard_map/ppermute | solution.py:67
  68.5 42.3 %collective-permute-start.22 = (bf16[4,48,768]{2,1,0:T(8,128)(2,1)S(1)}, bf16[4,48,768]{2,1,0:T(8,128)(2,1)S(1)}, u32[]{:S(2)}, u32[]{:S(2)}) collective-permute-start(bf16[4,48,768]{2,1,0:T(8,128)(2,1)S(1)} %get-tuple-element.155.refs_0_), channel_id=1, source_target_pairs={{0,2},{2,0},{4,6},{6,4},{8,10},{10,8},{12,14},{14,12},{16,18},{18,... | collective-permute-start | bytes 884744 | tf_op jit(solution)/shard_map/ppermute | solution.py:67
  76.4 34.5 %collective-permute-start.26 = (bf16[4,48,768]{2,1,0:T(8,128)(2,1)S(1)}, bf16[4,48,768]{2,1,0:T(8,128)(2,1)S(1)}, u32[]{:S(2)}, u32[]{:S(2)}) collective-permute-start(bf16[4,48,768]{2,1,0:T(8,128)(2,1)S(1)} %get-tuple-element.156.refs_4_), channel_id=1, source_target_pairs={{0,4},{2,6},{4,0},{6,2},{8,12},{10,14},{12,8},{14,10},{16,20},{18,... | collective-permute-start | bytes 884744 | tf_op jit(solution)/shard_map/ppermute | solution.py:67
  76.7 35.1 %collective-permute-start.32 = (bf16[4,48,768]{2,1,0:T(8,128)(2,1)S(1)}, bf16[4,48,768]{2,1,0:T(8,128)(2,1)S(1)}, u32[]{:S(2)}, u32[]{:S(2)}) collective-permute-start(bf16[4,48,768]{2,1,0:T(8,128)(2,1)S(1)} %get-tuple-element.158.refs_0_), channel_id=1, source_target_pairs={{0,4},{2,6},{4,0},{6,2},{8,12},{10,14},{12,8},{14,10},{16,20},{18,... | collective-permute-start | bytes 884744 | tf_op jit(solution)/shard_map/ppermute | solution.py:67
  83.4 34.2 %collective-permute-start.31 = (bf16[4,48,768]{2,1,0:T(8,128)(2,1)S(1)}, bf16[4,48,768]{2,1,0:T(8,128)(2,1)}, u32[]{:S(2)}, u32[]{:S(2)}) collective-permute-start(bf16[4,48,768]{2,1,0:T(8,128)(2,1)S(1)} %get-tuple-element.158.refs_0_), channel_id=1, source_target_pairs={{0,2},{2,0},{4,6},{6,4},{8,10},{10,8},{12,14},{14,12},{16,18},{18,... | collective-permute-start | bytes 884744 | tf_op jit(solution)/shard_map/ppermute | solution.py:67
  87.3 26.5 %collective-permute-start.34 = (bf16[4,48,768]{2,1,0:T(8,128)(2,1)S(1)}, bf16[4,48,768]{2,1,0:T(8,128)(2,1)}, u32[]{:S(2)}, u32[]{:S(2)}) collective-permute-start(bf16[4,48,768]{2,1,0:T(8,128)(2,1)S(1)} %get-tuple-element.159.refs_4_), channel_id=1, source_target_pairs={{0,2},{2,0},{4,6},{6,4},{8,10},{10,8},{12,14},{14,12},{16,18},{18,... | collective-permute-start | bytes 884744 | tf_op jit(solution)/shard_map/ppermute | solution.py:67
  110.7 28.5 %collective-permute-start.38 = (bf16[512,768]{1,0:T(8,128)(2,1)}, bf16[512,768]{1,0:T(8,128)(2,1)}, u32[]{:S(2)}, u32[]{:S(2)}) collective-permute-start(bf16[512,768]{1,0:T(8,128)(2,1)} %outward.5.refs_0_), channel_id=1, source_target_pairs={{0,1},{1,0},{2,3},{3,2},{4,5},{5,4},{6,7},{7,6},{8,9},{9,8},{10,11... | collective-permute-start | bytes 2359304 | tf_op jit(solution)/shard_map/ppermute | solution.py:71
  113.8 12.8 %collective-permute-start.27 = (bf16[4,48,768]{2,1,0:T(8,128)(2,1)S(1)}, bf16[4,48,768]{2,1,0:T(8,128)(2,1)S(1)}, u32[]{:S(2)}, u32[]{:S(2)}) collective-permute-start(bf16[4,48,768]{2,1,0:T(8,128)(2,1)S(1)} %collective-permute-done.25.refs_5_), channel_id=1, source_target_pairs={{0,4},{2,6},{4,0},{6,2},{8,12},{10,14},{12,8},{14,10},{16,20},{18,... | collective-permute-start | bytes 884744 | tf_op jit(solution)/shard_map/ppermute | solution.py:67
  117.6 31.4 %collective-permute-start.37 = (bf16[512,768]{1,0:T(8,128)(2,1)}, bf16[512,768]{1,0:T(8,128)(2,1)S(1)}, u32[]{:S(2)}, u32[]{:S(2)}) collective-permute-start(bf16[512,768]{1,0:T(8,128)(2,1)} %outward.4.mine_ref), channel_id=1, source_target_pairs={{0,1},{1,0},{2,3},{3,2},{4,5},{5,4},{6,7},{7,6},{8,9},{9,8},{10,11... | collective-permute-start | bytes 2359304 | tf_op jit(solution)/shard_map/ppermute | solution.py:71
  120.8 39.4 %collective-permute-start.18 = (bf16[512,768]{1,0:T(8,128)(2,1)}, bf16[512,768]{1,0:T(8,128)(2,1)S(1)}, u32[]{:S(2)}, u32[]{:S(2)}) collective-permute-start(bf16[512,768]{1,0:T(8,128)(2,1)} %outward.3.mine_ref), channel_id=1, source_target_pairs={{0,1},{1,0},{2,3},{3,2},{4,5},{5,4},{6,7},{7,6},{8,9},{9,8},{10,11... | collective-permute-start | bytes 2359304 | tf_op jit(solution)/shard_map/ppermute | solution.py:71
  121.1 11.4 %collective-permute-start.33 = (bf16[4,48,768]{2,1,0:T(8,128)(2,1)S(1)}, bf16[4,48,768]{2,1,0:T(8,128)(2,1)S(1)}, u32[]{:S(2)}, u32[]{:S(2)}) collective-permute-start(bf16[4,48,768]{2,1,0:T(8,128)(2,1)S(1)} %collective-permute-done.32.refs_2_), channel_id=1, source_target_pairs={{0,2},{2,0},{4,6},{6,4},{8,10},{10,8},{12,14},{14,12},{16,18},{18,... | collective-permute-start | bytes 884744 | tf_op jit(solution)/shard_map/ppermute | solution.py:67
  149.0 24.4 %collective-permute-start.41 = (bf16[512,768]{1,0:T(8,128)(2,1)}, bf16[512,768]{1,0:T(8,128)(2,1)S(1)}, u32[]{:S(2)}, u32[]{:S(2)}) collective-permute-start(bf16[512,768]{1,0:T(8,128)(2,1)} %get-tuple-element.174.refs_0_), channel_id=1, source_target_pairs={{0,1},{1,0},{2,3},{3,2},{4,5},{5,4},{6,7},{7,6},{8,9},{9,8},{10,11... | collective-permute-start | bytes 2359304 | tf_op jit(solution)/shard_map/ppermute | solution.py:71
  159.6 25.9 %collective-permute-start.40 = (bf16[512,768]{1,0:T(8,128)(2,1)}, bf16[512,768]{1,0:T(8,128)(2,1)S(1)}, u32[]{:S(2)}, u32[]{:S(2)}) collective-permute-start(bf16[512,768]{1,0:T(8,128)(2,1)} %get-tuple-element.173.mine_ref), channel_id=1, source_target_pairs={{0,1},{1,0},{2,3},{3,2},{4,5},{5,4},{6,7},{7,6},{8,9},{9,8},{10,11... | collective-permute-start | bytes 2359304 | tf_op jit(solution)/shard_map/ppermute | solution.py:71
  171.4 26.0 %collective-permute-start.39 = (bf16[512,768]{1,0:T(8,128)(2,1)}, bf16[512,768]{1,0:T(8,128)(2,1)S(1)}, u32[]{:S(2)}, u32[]{:S(2)}) collective-permute-start(bf16[512,768]{1,0:T(8,128)(2,1)} %get-tuple-element.170.mine_ref), channel_id=1, source_target_pairs={{0,1},{1,0},{2,3},{3,2},{4,5},{5,4},{6,7},{7,6},{8,9},{9,8},{10,11... | collective-permute-start | bytes 2359304 | tf_op jit(solution)/shard_map/ppermute | solution.py:71
  185.1 67.5 %collective-permute-start.44 = (bf16[512,768]{1,0:T(8,128)(2,1)}, bf16[512,768]{1,0:T(8,128)(2,1)S(1)}, u32[]{:S(2)}, u32[]{:S(2)}) collective-permute-start(bf16[512,768]{1,0:T(8,128)(2,1)} %get-tuple-element.190.refs_0_), channel_id=1, source_target_pairs={{0,1},{1,0},{2,3},{3,2},{4,5},{5,4},{6,7},{7,6},{8,9},{9,8},{10,11... | collective-permute-start | bytes 2359304 | tf_op jit(solution)/shard_map/ppermute | solution.py:71
  197.3 61.5 %collective-permute-start.43 = (bf16[512,768]{1,0:T(8,128)(2,1)}, bf16[512,768]{1,0:T(8,128)(2,1)S(1)}, u32[]{:S(2)}, u32[]{:S(2)}) collective-permute-start(bf16[512,768]{1,0:T(8,128)(2,1)} %get-tuple-element.189.mine_ref), channel_id=1, source_target_pairs={{0,1},{1,0},{2,3},{3,2},{4,5},{5,4},{6,7},{7,6},{8,9},{9,8},{10,11... | collective-permute-start | bytes 2359304 | tf_op jit(solution)/shard_map/ppermute | solution.py:71
  218.8 16.5 %collective-permute-start.84 = (bf16[2,4,48,768]{3,2,1,0:T(8,128)(2,1)}, bf16[2,4,48,768]{3,2,1,0:T(8,128)(2,1)}, u32[]{:S(2)}, u32[]{:S(2)}) collective-permute-start(bf16[2,4,48,768]{3,2,1,0:T(8,128)(2,1)} %get-tuple-element.255), channel_id=1, source_target_pairs={{0,4},{2,6},{4,0},{6,2},{8,12},{10,14},{12,8},{14,10},{16,20},{18,... | collective-permute-start | bytes 1769480 | tf_op jit(solution)/shard_map/ppermute | solution.py:67
  219.6 19.4 %collective-permute-start.83 = (bf16[2,4,48,768]{3,2,1,0:T(8,128)(2,1)}, bf16[2,4,48,768]{3,2,1,0:T(8,128)(2,1)}, u32[]{:S(2)}, u32[]{:S(2)}) collective-permute-start(bf16[2,4,48,768]{3,2,1,0:T(8,128)(2,1)} %get-tuple-element.253), channel_id=1, source_target_pairs={{0,2},{2,0},{4,6},{6,4},{8,10},{10,8},{12,14},{14,12},{16,18},{18,... | collective-permute-start | bytes 1769480 | tf_op jit(solution)/shard_map/ppermute | solution.py:67
  231.3 16.0 %collective-permute-start.77 = (bf16[2,4,48,768]{3,2,1,0:T(8,128)(2,1)}, bf16[2,4,48,768]{3,2,1,0:T(8,128)(2,1)S(1)}, u32[]{:S(2)}, u32[]{:S(2)}) collective-permute-start(bf16[2,4,48,768]{3,2,1,0:T(8,128)(2,1)} %get-tuple-element.244), channel_id=1, source_target_pairs={{0,4},{2,6},{4,0},{6,2},{8,12},{10,14},{12,8},{14,10},{16,20},{18,... | collective-permute-start | bytes 1769480 | tf_op jit(solution)/shard_map/ppermute | solution.py:67
  235.3 14.8 %collective-permute-start.76 = (bf16[2,4,48,768]{3,2,1,0:T(8,128)(2,1)}, bf16[2,4,48,768]{3,2,1,0:T(8,128)(2,1)S(1)}, u32[]{:S(2)}, u32[]{:S(2)}) collective-permute-start(bf16[2,4,48,768]{3,2,1,0:T(8,128)(2,1)} %get-tuple-element.242), channel_id=1, source_target_pairs={{0,2},{2,0},{4,6},{6,4},{8,10},{10,8},{12,14},{14,12},{16,18},{18,... | collective-permute-start | bytes 1769480 | tf_op jit(solution)/shard_map/ppermute | solution.py:67
  239.0 26.0 %collective-permute-start.42 = (bf16[512,768]{1,0:T(8,128)(2,1)S(1)}, bf16[512,768]{1,0:T(8,128)(2,1)S(1)}, u32[]{:S(2)}, u32[]{:S(2)}) collective-permute-start(bf16[512,768]{1,0:T(8,128)(2,1)S(1)} %copy-done.12), channel_id=1, source_target_pairs={{0,1},{1,0},{2,3},{3,2},{4,5},{5,4},{6,7},{7,6},{8,9},{9,8},{10,11... | collective-permute-start | bytes 2359304 | tf_op jit(solution)/shard_map/ppermute | solution.py:71
  247.4 97.0 %collective-permute-start.85 = (bf16[4,48,768]{2,1,0:T(8,128)(2,1)}, bf16[4,48,768]{2,1,0:T(8,128)(2,1)S(1)}, u32[]{:S(2)}, u32[]{:S(2)}) collective-permute-start(bf16[4,48,768]{2,1,0:T(8,128)(2,1)} %fusion.3), channel_id=1, source_target_pairs={{0,4},{2,6},{4,0},{6,2},{8,12},{10,14},{12,8},{14,10},{16,20},{18,... | collective-permute-start | bytes 884744 | tf_op jit(solution)/shard_map/ppermute | solution.py:67
  250.1 94.4 %collective-permute-start.86 = (bf16[4,48,768]{2,1,0:T(8,128)(2,1)}, bf16[4,48,768]{2,1,0:T(8,128)(2,1)}, u32[]{:S(2)}, u32[]{:S(2)}) collective-permute-start(bf16[4,48,768]{2,1,0:T(8,128)(2,1)} %fusion.2), channel_id=1, source_target_pairs={{0,2},{2,0},{4,6},{6,4},{8,10},{10,8},{12,14},{14,12},{16,18},{18,... | collective-permute-start | bytes 884744 | tf_op jit(solution)/shard_map/ppermute | solution.py:67
  323.8 10.7 %collective-permute-start.92 = (f32[432]{0:T(512)S(1)}, f32[432]{0:T(512)S(1)}, u32[]{:S(2)}, u32[]{:S(2)}) collective-permute-start(f32[432]{0:T(512)S(1)} %bitcast.301), channel_id=1, source_target_pairs={{0,8},{2,10},{4,12},{6,14},{8,0},{10,2},{12,4},{14,6},{16,24},{18,... | collective-permute-start | bytes 5192 | tf_op jit(solution)/shard_map/ppermute | solution.py:67
  323.9 11.6 %collective-permute-start.93 = (f32[432]{0:T(512)S(1)}, f32[432]{0:T(512)S(1)}, u32[]{:S(2)}, u32[]{:S(2)}) collective-permute-start(f32[432]{0:T(512)S(1)} %bitcast.300), channel_id=1, source_target_pairs={{0,16},{2,18},{4,20},{6,22},{8,24},{10,26},{12,28},{14,30},{16,0},... | collective-permute-start | bytes 5192 | tf_op jit(solution)/shard_map/ppermute | solution.py:67
  326.3 11.0 %collective-permute-start.94 = (f32[432]{0:T(512)S(1)}, f32[432]{0:T(512)S(1)}, u32[]{:S(2)}, u32[]{:S(2)}) collective-permute-start(f32[432]{0:T(512)S(1)} %bitcast.299), channel_id=1, source_target_pairs={{0,24},{2,26},{4,28},{6,30},{8,16},{10,18},{12,20},{14,22},{16,8},... | collective-permute-start | bytes 5192 | tf_op jit(solution)/shard_map/ppermute | solution.py:67
  334.5 12.5 %collective-permute-start.78 = (bf16[4,48,768]{2,1,0:T(8,128)(2,1)S(1)}, bf16[4,48,768]{2,1,0:T(8,128)(2,1)S(1)}, u32[]{:S(2)}, u32[]{:S(2)}) collective-permute-start(bf16[4,48,768]{2,1,0:T(8,128)(2,1)S(1)} %copy-done.45), channel_id=1, source_target_pairs={{0,4},{2,6},{4,0},{6,2},{8,12},{10,14},{12,8},{14,10},{16,20},{18,... | collective-permute-start | bytes 884744 | tf_op jit(solution)/shard_map/ppermute | solution.py:67
  335.5 13.4 %collective-permute-start.79 = (bf16[4,48,768]{2,1,0:T(8,128)(2,1)S(1)}, bf16[4,48,768]{2,1,0:T(8,128)(2,1)S(1)}, u32[]{:S(2)}, u32[]{:S(2)}) collective-permute-start(bf16[4,48,768]{2,1,0:T(8,128)(2,1)S(1)} %copy-done.44), channel_id=1, source_target_pairs={{0,2},{2,0},{4,6},{6,4},{8,10},{10,8},{12,14},{14,12},{16,18},{18,... | collective-permute-start | bytes 884744 | tf_op jit(solution)/shard_map/ppermute | solution.py:67
  337.3 13.4 %collective-permute-start.70 = (bf16[2,4,48,128]{3,2,1,0:T(8,128)(2,1)}, bf16[2,4,48,128]{3,2,1,0:T(8,128)(2,1)}, u32[]{:S(2)}, u32[]{:S(2)}) collective-permute-start(bf16[2,4,48,128]{3,2,1,0:T(8,128)(2,1)} %get-tuple-element.233), channel_id=1, source_target_pairs={{0,4},{2,6},{4,0},{6,2},{8,12},{10,14},{12,8},{14,10},{16,20},{18,... | collective-permute-start | bytes 294920 | tf_op jit(solution)/shard_map/ppermute | solution.py:67
  344.3 12.8 %collective-permute-start.69 = (bf16[2,4,48,256]{3,2,1,0:T(8,128)(2,1)}, bf16[2,4,48,256]{3,2,1,0:T(8,128)(2,1)S(1)}, u32[]{:S(2)}, u32[]{:S(2)}) collective-permute-start(bf16[2,4,48,256]{3,2,1,0:T(8,128)(2,1)} %get-tuple-element.231), channel_id=1, source_target_pairs={{0,2},{2,0},{4,6},{6,4},{8,10},{10,8},{12,14},{14,12},{16,18},{18,... | collective-permute-start | bytes 589832 | tf_op jit(solution)/shard_map/ppermute | solution.py:67
  347.0 10.8 %collective-permute-start.48 = (bf16[2,4,48,256]{3,2,1,0:T(8,128)(2,1)S(1)}, bf16[2,4,48,256]{3,2,1,0:T(8,128)(2,1)S(1)}, u32[]{:S(2)}, u32[]{:S(2)}) collective-permute-start(bf16[2,4,48,256]{3,2,1,0:T(8,128)(2,1)S(1)} %copy-done.91), channel_id=1, source_target_pairs={{0,2},{2,0},{4,6},{6,4},{8,10},{10,8},{12,14},{14,12},{16,18},{18,... | collective-permute-start | bytes 589832 | tf_op jit(solution)/shard_map/ppermute | solution.py:67
  357.1 67.1 %collective-permute-start.45 = (bf16[512,768]{1,0:T(8,128)(2,1)S(1)}, bf16[512,768]{1,0:T(8,128)(2,1)S(1)}, u32[]{:S(2)}, u32[]{:S(2)}) collective-permute-start(bf16[512,768]{1,0:T(8,128)(2,1)S(1)} %copy-done), channel_id=1, source_target_pairs={{0,1},{1,0},{2,3},{3,2},{4,5},{5,4},{6,7},{7,6},{8,9},{9,8},{10,11... | collective-permute-start | bytes 2359304 | tf_op jit(solution)/shard_map/ppermute | solution.py:71
  357.2 67.2 %collective-permute-start.46 = (bf16[512,768]{1,0:T(8,128)(2,1)S(1)}, bf16[512,768]{1,0:T(8,128)(2,1)S(1)}, u32[]{:S(2)}, u32[]{:S(2)}) collective-permute-start(bf16[512,768]{1,0:T(8,128)(2,1)S(1)} %copy-done.1), channel_id=1, source_target_pairs={{0,1},{1,0},{2,3},{3,2},{4,5},{5,4},{6,7},{7,6},{8,9},{9,8},{10,11... | collective-permute-start | bytes 2359304 | tf_op jit(solution)/shard_map/ppermute | solution.py:71
  357.8 21.5 %collective-permute-start.87 = (bf16[48,1536]{1,0:T(8,128)(2,1)S(1)}, bf16[48,1536]{1,0:T(8,128)(2,1)S(1)}, u32[]{:S(2)}, u32[]{:S(2)}) collective-permute-start(bf16[48,1536]{1,0:T(8,128)(2,1)S(1)} %pad_maximum_fusion.8), channel_id=1, source_target_pairs={{0,8},{2,10},{4,12},{6,14},{8,0},{10,2},{12,4},{14,6},{16,24},{18,... | collective-permute-start | bytes 442376 | tf_op jit(solution)/shard_map/ppermute | solution.py:67
  358.7 20.7 %collective-permute-start.88 = (bf16[48,1536]{1,0:T(8,128)(2,1)S(1)}, bf16[48,1536]{1,0:T(8,128)(2,1)S(1)}, u32[]{:S(2)}, u32[]{:S(2)}) collective-permute-start(bf16[48,1536]{1,0:T(8,128)(2,1)S(1)} %pad_maximum_fusion.9), channel_id=1, source_target_pairs={{0,16},{2,18},{4,20},{6,22},{8,24},{10,26},{12,28},{14,30},{16,0},... | collective-permute-start | bytes 442376 | tf_op jit(solution)/shard_map/ppermute | solution.py:67
  379.4 11.6 %collective-permute-start.81 = (bf16[48,1536]{1,0:T(8,128)(2,1)S(1)}, bf16[48,1536]{1,0:T(8,128)(2,1)S(1)}, u32[]{:S(2)}, u32[]{:S(2)}) collective-permute-start(bf16[48,1536]{1,0:T(8,128)(2,1)S(1)} %pad_maximum_fusion.6), channel_id=1, source_target_pairs={{0,16},{2,18},{4,20},{6,22},{8,24},{10,26},{12,28},{14,30},{16,0},... | collective-permute-start | bytes 442376 | tf_op jit(solution)/shard_map/ppermute | solution.py:67
  (143 other events, 1461.4 us)
